TPU v7x, 32 devices: a whole 2x2x4 slice. The times are simulated.
32 devices in a mesh: dp: 16 (over z, y, core), fsdp: 2 (over x).
Axes of the slice: x: 2, y: 2, z: 4, core: 2. Of those that a mesh axis runs over, the one named last changes fastest.
Arguments:
- text_tokens: bfloat16 [18432, 768], P(('dp', 'fsdp')), may hold values from -6 to 6
- image_tokens: bfloat16 [57600, 768], P(('dp', 'fsdp')), may hold values from -6 to 6
- pair_counts: int32 [32], replicated, may hold values from 9 to 36, as said below
- log_scale: float32 [1], replicated, may hold values from 3.7 to 4.1
- text_gain: bfloat16 [768], P('fsdp'), may hold values from 0.25 to 1.75
- text_offset: bfloat16 [768], P('fsdp'), may hold values from -1.1953125 to 1.1953125
- text_joint: bfloat16 [768, 2304], P('fsdp'), may hold values from -0.21875 to 0.21875
- text_mixer: bfloat16 [768, 768], P('fsdp'), may hold values from -0.4375 to 0.4375
- text_mixbias: bfloat16 [768], P('fsdp'), may hold values from -1.1953125 to 1.1953125
- text_feedgain: bfloat16 [768], P('fsdp'), may hold values from 0.25 to 1.75
- text_feedoffset: bfloat16 [768], P('fsdp'), may hold values from -1.1953125 to 1.1953125
- text_upward: bfloat16 [768, 3072], P('fsdp'), may hold values from -0.21875 to 0.21875
- text_upbias: bfloat16 [3072], P('fsdp'), may hold values from -1.1953125 to 1.1953125
- text_downward: bfloat16 [3072, 768], P('fsdp'), may hold values from -0.109375 to 0.109375
- text_downbias: bfloat16 [768], P('fsdp'), may hold values from -1.1953125 to 1.1953125
- text_endgain: bfloat16 [768], P('fsdp'), may hold values from 0.25 to 1.75
- text_endoffset: bfloat16 [768], P('fsdp'), may hold values from -1.1953125 to 1.1953125
- text_project: bfloat16 [768, 768], P('fsdp'), may hold values from -0.21875 to 0.21875
- image_gain: bfloat16 [768], replicated, may hold values from 0.25 to 1.75
- image_offset: bfloat16 [768], replicated, may hold values from -1.1953125 to 1.1953125
- image_joint: bfloat16 [768, 2304], replicated, may hold values from -0.21875 to 0.21875
- image_mixer: bfloat16 [768, 768], replicated, may hold values from -0.5 to 0.5
- image_mixbias: bfloat16 [768], replicated, may hold values from -1.1953125 to 1.1953125
- image_feedgain: bfloat16 [768], replicated, may hold values from 0.25 to 1.75
- image_feedoffset: bfloat16 [768], replicated, may hold values from -1.1953125 to 1.1953125
- image_upward: bfloat16 [768, 3072], replicated, may hold values from -0.21875 to 0.21875
- image_upbias: bfloat16 [3072], replicated, may hold values from -1.1953125 to 1.1953125
- image_downward: bfloat16 [3072, 768], replicated, may hold values from -0.109375 to 0.109375
- image_downbias: bfloat16 [768], replicated, may hold values from -1.1953125 to 1.1953125
- image_endgain: bfloat16 [768], replicated, may hold values from 0.25 to 1.75
- image_endoffset: bfloat16 [768], replicated, may hold values from -1.1953125 to 1.1953125
- image_project: bfloat16 [768, 768], replicated, may hold values from -0.21875 to 0.21875
Outputs:
- grad_gain: float32 [768], P('fsdp')
- grad_offset: float32 [768], P('fsdp')
- grad_joint: float32 [768, 2304], P('fsdp')
- grad_mixer: float32 [768, 768], P('fsdp')
- grad_mixbias: float32 [768], P('fsdp')
- grad_feedgain: float32 [768], P('fsdp')
- grad_feedoffset: float32 [768], P('fsdp')
- grad_upward: float32 [768, 3072], P('fsdp')
- grad_upbias: float32 [3072], P('fsdp')
- grad_downward: float32 [3072, 768], P('fsdp')
- grad_downbias: float32 [768], P('fsdp')
- grad_endgain: float32 [768], P('fsdp')
- grad_endoffset: float32 [768], P('fsdp')
- grad_project: float32 [768, 768], P('fsdp')
- grad_scale: float32 [1], replicated
- grad_tokens: float32 [18432, 768], P(('dp', 'fsdp'))
- loss_value: float32 [1], replicated
Inputs may be any that keep to these rules, and one draw needn't show every extreme that they name: `pair_counts`: each count is 36 divided by 1, 2, 3 or 4, rounded down; some device holds 36 live pairs; live pairs take a device's first slots.
All inputs are finite; a program needn't handle non-finite values.
Results may differ from a plain program's by a relative error of at most 0.018.
Values may be sent and summed in bfloat16 or wider, within the bound.
A program may use at most 136 MiB of HBM per device.

v0:
```python
import jax
import jax.numpy as jnp
from jax import lax
from jax.sharding import PartitionSpec as P

HEADS = 12
HEAD_DIM = 64
TEXT_LEN = 16
IMAGE_LEN = 50
PER_BATCH = 12
BATCHES = 3
SLOTS = 36


EPSILON = 1e-06


def product(left_side, right_side):
    return jnp.dot(left_side, right_side, preferred_element_type=jnp.float32)


def contract_last(left_side, right_side):
    return lax.dot_general(
        left_side, right_side, (((1,), (1,)), ((), ())), preferred_element_type=jnp.float32
    )


def contract_first(left_side, right_side):
    return lax.dot_general(
        left_side, right_side, (((0,), (0,)), ((), ())), preferred_element_type=jnp.float32
    )


def layer_norm(values, gain_vector, offset):
    centred = values - jnp.mean(values, axis=-1, keepdims=True)
    variance = jnp.mean(centred * centred, axis=-1, keepdims=True)
    return centred * lax.rsqrt(variance + EPSILON) * gain_vector.astype(
        jnp.float32
    ) + offset.astype(jnp.float32)


def normalize(embedding):
    return embedding * lax.rsqrt(jnp.sum(embedding * embedding, axis=-1, keepdims=True) + EPSILON)


def forward_block(tokens, weights, length):
    (
        norm_gain,
        norm_offset,
        joint_weight,
        mixer_weight,
        mixer_bias,
        feed_gain,
        feed_offset,
        up_weight,
        up_bias,
        down_weight,
        down_bias,
        end_gain,
        end_offset,
        projection,
    ) = weights
    inputs = tokens.astype(jnp.float32)
    total_rows, model_width = inputs.shape
    seq_count = total_rows // length
    factor = HEAD_DIM ** (-0.5)
    normed = layer_norm(inputs, norm_gain, norm_offset).astype(jnp.bfloat16)
    triple = (
        product(normed, joint_weight)
        .astype(jnp.bfloat16)
        .reshape(seq_count, length, 3, HEADS, HEAD_DIM)
    )
    queries = triple[:, :, 0]
    keyset = triple[:, :, 1]
    valueset = triple[:, :, 2]
    scores = (
        jnp.einsum("sqhd,skhd->shqk", queries, keyset, preferred_element_type=jnp.float32) * factor
    )
    soft_weights = jax.nn.softmax(scores, axis=-1)
    soft_low = soft_weights.astype(jnp.bfloat16)
    attended = jnp.einsum("shqk,skhd->sqhd", soft_low, valueset, preferred_element_type=jnp.float32)
    attended = attended.reshape(total_rows, model_width).astype(jnp.bfloat16)
    residual = inputs + product(attended, mixer_weight) + mixer_bias.astype(jnp.float32)
    normed_two = layer_norm(residual, feed_gain, feed_offset).astype(jnp.bfloat16)
    pre_active = product(normed_two, up_weight) + up_bias.astype(jnp.float32)
    active = jax.nn.gelu(pre_active).astype(jnp.bfloat16)
    output = residual + product(active, down_weight) + down_bias.astype(jnp.float32)
    final_norm = layer_norm(output, end_gain, end_offset)
    pooled = jnp.mean(final_norm.reshape(seq_count, length, model_width), axis=1)
    embedding = product(pooled.astype(jnp.bfloat16), projection)
    unit_vector = normalize(embedding)
    kept_values = (
        inputs,
        normed,
        triple,
        soft_weights,
        soft_low,
        attended,
        residual,
        normed_two,
        pre_active,
        active,
        output,
        pooled,
        embedding,
    )
    return (unit_vector, kept_values)


def backward_block(kept_values, weights, unit_grad, length):
    (
        norm_gain,
        norm_offset,
        joint_weight,
        mixer_weight,
        mixer_bias,
        feed_gain,
        feed_offset,
        up_weight,
        up_bias,
        down_weight,
        down_bias,
        end_gain,
        end_offset,
        projection,
    ) = weights
    (
        inputs,
        normed,
        triple,
        soft_weights,
        soft_low,
        attended,
        residual,
        normed_two,
        pre_active,
        active,
        output,
        pooled,
        embedding,
    ) = kept_values
    total_rows, model_width = inputs.shape
    seq_count = total_rows // length
    factor = HEAD_DIM ** (-0.5)
    unused_unit, norm_back = jax.vjp(normalize, embedding)
    embed_grad = norm_back(unit_grad)[0].astype(jnp.bfloat16)
    project_grad = contract_first(pooled.astype(jnp.bfloat16), embed_grad)
    pooled_grad = contract_last(embed_grad, projection)
    final_grad = jnp.broadcast_to(
        pooled_grad[:, None, :] / length, (seq_count, length, model_width)
    ).reshape(total_rows, model_width)
    unused_final, end_back = jax.vjp(
        layer_norm, output, end_gain.astype(jnp.float32), end_offset.astype(jnp.float32)
    )
    output_grad, endgain_grad, endoffset_grad = end_back(final_grad)
    down_low = output_grad.astype(jnp.bfloat16)
    downbias_grad = jnp.sum(output_grad, axis=0)
    downward_grad = contract_first(active, down_low)
    active_grad = contract_last(down_low, down_weight)
    unused_active, gelu_back = jax.vjp(jax.nn.gelu, pre_active)
    pre_grad = gelu_back(active_grad)[0]
    upbias_grad = jnp.sum(pre_grad, axis=0)
    pre_low = pre_grad.astype(jnp.bfloat16)
    upward_grad = contract_first(normed_two, pre_low)
    normed_grad = contract_last(pre_low, up_weight)
    unused_feed, feed_back = jax.vjp(
        layer_norm, residual, feed_gain.astype(jnp.float32), feed_offset.astype(jnp.float32)
    )
    residual_part, feedgain_grad, feedoffset_grad = feed_back(normed_grad)
    residual_grad = output_grad + residual_part
    mixbias_grad = jnp.sum(residual_grad, axis=0)
    mix_low = residual_grad.astype(jnp.bfloat16)
    mixer_grad = contract_first(attended, mix_low)
    attended_grad = contract_last(mix_low, mixer_weight).astype(jnp.bfloat16)
    attended_grad = attended_grad.reshape(seq_count, length, HEADS, HEAD_DIM)
    queries = triple[:, :, 0]
    keyset = triple[:, :, 1]
    valueset = triple[:, :, 2]
    soft_grad = jnp.einsum(
        "sqhd,skhd->shqk", attended_grad, valueset, preferred_element_type=jnp.float32
    )
    value_grad = jnp.einsum(
        "shqk,sqhd->skhd", soft_low, attended_grad, preferred_element_type=jnp.float32
    )
    score_grad = soft_weights * (
        soft_grad - jnp.sum(soft_weights * soft_grad, axis=-1, keepdims=True)
    )
    score_grad = score_grad.astype(jnp.bfloat16)
    query_grad = (
        jnp.einsum("shqk,skhd->sqhd", score_grad, keyset, preferred_element_type=jnp.float32)
        * factor
    )
    key_grad = (
        jnp.einsum("shqk,sqhd->skhd", score_grad, queries, preferred_element_type=jnp.float32)
        * factor
    )
    triple_grad = jnp.stack([query_grad, key_grad, value_grad], axis=2)
    triple_grad = triple_grad.reshape(total_rows, 3 * model_width).astype(jnp.bfloat16)
    joint_grad = contract_first(normed, triple_grad)
    first_grad = contract_last(triple_grad, joint_weight)
    unused_first, first_back = jax.vjp(
        layer_norm, inputs, norm_gain.astype(jnp.float32), norm_offset.astype(jnp.float32)
    )
    input_part, gain_grad, offset_grad = first_back(first_grad)
    input_grad = residual_grad + input_part
    grad_terms = (
        gain_grad,
        offset_grad,
        joint_grad,
        mixer_grad,
        mixbias_grad,
        feedgain_grad,
        feedoffset_grad,
        upward_grad,
        upbias_grad,
        downward_grad,
        downbias_grad,
        endgain_grad,
        endoffset_grad,
        project_grad,
    )
    return (grad_terms, input_grad)


def on_device(
    text_tokens,
    image_tokens,
    pair_counts,
    log_scale,
    text_gain,
    text_offset,
    text_joint,
    text_mixer,
    text_mixbias,
    text_feedgain,
    text_feedoffset,
    text_upward,
    text_upbias,
    text_downward,
    text_downbias,
    text_endgain,
    text_endoffset,
    text_project,
    image_gain,
    image_offset,
    image_joint,
    image_mixer,
    image_mixbias,
    image_feedgain,
    image_feedoffset,
    image_upward,
    image_upbias,
    image_downward,
    image_downbias,
    image_endgain,
    image_endoffset,
    image_project,
):
    image_weights = (
        image_gain,
        image_offset,
        image_joint,
        image_mixer,
        image_mixbias,
        image_feedgain,
        image_feedoffset,
        image_upward,
        image_upbias,
        image_downward,
        image_downbias,
        image_endgain,
        image_endoffset,
        image_project,
    )
    group_count = lax.axis_size("dp") * lax.axis_size("fsdp")
    device = lax.axis_index("dp") * lax.axis_size("fsdp") + lax.axis_index("fsdp")
    pair_total = group_count * SLOTS
    live_all = (
        (jnp.arange(SLOTS)[None, :] < pair_counts[:, None]).astype(jnp.float32).reshape(pair_total)
    )
    live_total = jnp.sum(live_all)
    text_live = lax.dynamic_slice_in_dim(live_all, device * SLOTS, SLOTS)
    temper = jnp.exp(log_scale[0])
    half_inverse = 1.0 / (2.0 * live_total)
    batch_rows = PER_BATCH * TEXT_LEN
    image_unit, image_kept = forward_block(image_tokens, image_weights, IMAGE_LEN)
    image_low = image_unit.astype(jnp.bfloat16)
    unit_list = []
    for batch_index in range(BATCHES):
        weights_now = (
            lax.all_gather(text_gain, "fsdp", axis=0, tiled=True),
            lax.all_gather(text_offset, "fsdp", axis=0, tiled=True),
            lax.all_gather(text_joint, "fsdp", axis=0, tiled=True),
            lax.all_gather(text_mixer, "fsdp", axis=0, tiled=True),
            lax.all_gather(text_mixbias, "fsdp", axis=0, tiled=True),
            lax.all_gather(text_feedgain, "fsdp", axis=0, tiled=True),
            lax.all_gather(text_feedoffset, "fsdp", axis=0, tiled=True),
            lax.all_gather(text_upward, "fsdp", axis=0, tiled=True),
            lax.all_gather(text_upbias, "fsdp", axis=0, tiled=True),
            lax.all_gather(text_downward, "fsdp", axis=0, tiled=True),
            lax.all_gather(text_downbias, "fsdp", axis=0, tiled=True),
            lax.all_gather(text_endgain, "fsdp", axis=0, tiled=True),
            lax.all_gather(text_endoffset, "fsdp", axis=0, tiled=True),
            lax.all_gather(text_project, "fsdp", axis=0, tiled=True),
        )
        batch_tokens = text_tokens[batch_index * batch_rows : (batch_index + 1) * batch_rows]
        unit_list.append(forward_block(batch_tokens, weights_now, TEXT_LEN)[0])
    text_unit = jnp.concatenate(unit_list, axis=0)
    text_low = text_unit.astype(jnp.bfloat16)
    cosine = contract_last(text_low, lax.all_gather(image_low, ("dp", "fsdp"), axis=0, tiled=True))
    scaled = jnp.exp(temper * cosine - temper)
    image_live = live_all
    forward_row_sum = jnp.sum(scaled * image_live[None, :], axis=1)
    forward_column_sum = jnp.sum(scaled * text_live[:, None], axis=0)
    column_sum = forward_column_sum
    column_sum = lax.psum(column_sum, ("dp", "fsdp"))
    diagonal_cos = jnp.sum(text_low.astype(jnp.float32) * image_low.astype(jnp.float32), axis=1)
    row_log = temper + jnp.log(forward_row_sum)
    column_log = temper + jnp.log(lax.dynamic_slice_in_dim(column_sum, device * SLOTS, SLOTS))
    diagonal = temper * diagonal_cos
    loss_part = jnp.sum(text_live * (row_log - diagonal) + text_live * (column_log - diagonal)) / (
        2.0 * live_total
    )
    shard_piece = lax.all_gather(image_low, ("dp", "fsdp"), axis=0, tiled=True)
    cosine = contract_last(text_low, shard_piece)
    scaled = jnp.exp(temper * cosine - temper)
    image_live = live_all
    coupling = (
        scaled * (text_live / forward_row_sum)[:, None] * image_live[None, :]
        + scaled * text_live[:, None] * (image_live / column_sum)[None, :]
    ) * half_inverse
    temper_grad = jnp.sum(coupling * cosine)
    unit_grad = product((temper * coupling).astype(jnp.bfloat16), shard_piece)
    unit_grad, temper_grad = (unit_grad, temper_grad)
    unit_grad = unit_grad - temper / live_total * text_live[:, None] * image_low.astype(jnp.float32)
    temper_grad = temper_grad - jnp.sum(text_live * diagonal_cos) / live_total
    loss_total, scale_total = lax.psum((loss_part, temper * temper_grad), ("dp", "fsdp"))
    input_list = []
    shard_grads = None
    for batch_index in range(BATCHES):
        weights_now = (
            lax.all_gather(text_gain, "fsdp", axis=0, tiled=True),
            lax.all_gather(text_offset, "fsdp", axis=0, tiled=True),
            lax.all_gather(text_joint, "fsdp", axis=0, tiled=True),
            lax.all_gather(text_mixer, "fsdp", axis=0, tiled=True),
            lax.all_gather(text_mixbias, "fsdp", axis=0, tiled=True),
            lax.all_gather(text_feedgain, "fsdp", axis=0, tiled=True),
            lax.all_gather(text_feedoffset, "fsdp", axis=0, tiled=True),
            lax.all_gather(text_upward, "fsdp", axis=0, tiled=True),
            lax.all_gather(text_upbias, "fsdp", axis=0, tiled=True),
            lax.all_gather(text_downward, "fsdp", axis=0, tiled=True),
            lax.all_gather(text_downbias, "fsdp", axis=0, tiled=True),
            lax.all_gather(text_endgain, "fsdp", axis=0, tiled=True),
            lax.all_gather(text_endoffset, "fsdp", axis=0, tiled=True),
            lax.all_gather(text_project, "fsdp", axis=0, tiled=True),
        )
        batch_tokens = text_tokens[batch_index * batch_rows : (batch_index + 1) * batch_rows]
        unit_now, kept_values = forward_block(batch_tokens, weights_now, TEXT_LEN)
        grad_terms, input_grad = backward_block(
            kept_values,
            weights_now,
            unit_grad[batch_index * PER_BATCH : (batch_index + 1) * PER_BATCH],
            TEXT_LEN,
        )
        input_list.append(input_grad)
        batch_shards = (
            lax.psum_scatter(grad_terms[0], "fsdp", scatter_dimension=0, tiled=True),
            lax.psum_scatter(grad_terms[1], "fsdp", scatter_dimension=0, tiled=True),
            lax.psum_scatter(grad_terms[2], "fsdp", scatter_dimension=0, tiled=True),
            lax.psum_scatter(grad_terms[3], "fsdp", scatter_dimension=0, tiled=True),
            lax.psum_scatter(grad_terms[4], "fsdp", scatter_dimension=0, tiled=True),
            lax.psum_scatter(grad_terms[5], "fsdp", scatter_dimension=0, tiled=True),
            lax.psum_scatter(grad_terms[6], "fsdp", scatter_dimension=0, tiled=True),
            lax.psum_scatter(grad_terms[7], "fsdp", scatter_dimension=0, tiled=True),
            lax.psum_scatter(grad_terms[8], "fsdp", scatter_dimension=0, tiled=True),
            lax.psum_scatter(grad_terms[9], "fsdp", scatter_dimension=0, tiled=True),
            lax.psum_scatter(grad_terms[10], "fsdp", scatter_dimension=0, tiled=True),
            lax.psum_scatter(grad_terms[11], "fsdp", scatter_dimension=0, tiled=True),
            lax.psum_scatter(grad_terms[12], "fsdp", scatter_dimension=0, tiled=True),
            lax.psum_scatter(grad_terms[13], "fsdp", scatter_dimension=0, tiled=True),
        )
        shard_grads = (
            batch_shards
            if shard_grads is None
            else jax.tree.map(jnp.add, shard_grads, batch_shards)
        )
    final_grads = lax.psum(
        (
            shard_grads[0],
            shard_grads[1],
            shard_grads[2],
            shard_grads[3],
            shard_grads[4],
            shard_grads[5],
            shard_grads[6],
            shard_grads[7],
            shard_grads[8],
            shard_grads[9],
            shard_grads[10],
            shard_grads[11],
            shard_grads[12],
            shard_grads[13],
        ),
        "dp",
    )
    token_grad = jnp.concatenate(input_list, axis=0)
    return (
        final_grads[0],
        final_grads[1],
        final_grads[2],
        final_grads[3],
        final_grads[4],
        final_grads[5],
        final_grads[6],
        final_grads[7],
        final_grads[8],
        final_grads[9],
        final_grads[10],
        final_grads[11],
        final_grads[12],
        final_grads[13],
        jnp.reshape(scale_total, (1,)),
        token_grad,
        jnp.reshape(loss_total, (1,)),
    )


def solution(mesh):
    return jax.shard_map(
        on_device,
        mesh=mesh,
        in_specs=(
            P(("dp", "fsdp"), None),
            P(("dp", "fsdp"), None),
            P(),
            P(),
            P("fsdp"),
            P("fsdp"),
            P("fsdp", None),
            P("fsdp", None),
            P("fsdp"),
            P("fsdp"),
            P("fsdp"),
            P("fsdp", None),
            P("fsdp"),
            P("fsdp", None),
            P("fsdp"),
            P("fsdp"),
            P("fsdp"),
            P("fsdp", None),
            P(),
            P(),
            P(),
            P(),
            P(),
            P(),
            P(),
            P(),
            P(),
            P(),
            P(),
            P(),
            P(),
            P(),
        ),
        out_specs=(
            P("fsdp"),
            P("fsdp"),
            P("fsdp", None),
            P("fsdp", None),
            P("fsdp"),
            P("fsdp"),
            P("fsdp"),
            P("fsdp", None),
            P("fsdp"),
            P("fsdp", None),
            P("fsdp"),
            P("fsdp"),
            P("fsdp"),
            P("fsdp", None),
            P(),
            P(("dp", "fsdp"), None),
            P(),
        ),
        check_vma=False,
    )
```

profile of v0, /device:TPU:0, one launch (start us, length us, event | category | flops | bytes accessed | tf_op | source)
XLA Modules:
  0.0 1177.7 jit_solution(9616072995811261677)
XLA Ops:
  14.8 5.2 all-gather
  20.1 4.3 all-gather.1
  25.1 4.3 all-gather.2
  31.4 4.3 all-gather.3
  38.3 4.3 all-gather.4
  45.2 4.4 all-gather.5
  51.0 4.3 all-gather.6
  60.3 4.3 all-gather.7
  67.2 4.3 all-gather.8
  77.1 9.6 convolution_convert_fusion
  86.7 25.7 %reshape.524 = bf16[36,50,3,12,64]{4,3,2,1,0:T(8,128)(2,1)} reshape(bf16[1800,2304]{1,0:T(8,128)(2,1)} %convolution_convert_fusion) | data formatting | bytes 16588800 | tf_op jit(solution)/shard_map/reshape | solution.py:71
  112.4 15.2 %fusion.228 = (bf16[36,50,1,12,64]{4,3,2,1,0:T(8,128)(2,1)}, bf16[36,50,1,12,64]{4,3,2,1,0:T(8,128)(2,1)}, bf16[36,50,1,12,64]{4,3,2,1,0:T(8,128)(2,1)}) fusion(bf16[36,50,3,12,64]{4,3,2,1,0:T(8,128)(2,1)} %reshape.524), kind=kLoop, calls=%fused_computation.456 | loop fusion | bytes 16588800 | tf_op jit(solution)/shard_map/slice | solution.py:75
  127.6 13.1 %fusion.19 = f32[36,12,50,50]{2,3,1,0:T(8,128)} fusion(bf16[36,50,1,12,64]{4,3,2,1,0:T(8,128)(2,1)} %get-tuple-element.102, bf16[36,50,1,12,64]{4,3,2,1,0:T(8,128)(2,1)} %get-tuple-element.101), kind=kOutput, calls=%fused_computation.29 | convolution fusion | flops 138240000 | bytes 9849600 | tf_op jit(solution)/shard_map/sqhd,skhd->shqk/dot_general | solution.py:77
  140.7 16.1 %fusion.241 = (f32[36,12,50]{2,1,0:T(8,128)S(1)}, f32[36,12,50,50]{2,3,1,0:T(8,128)}) fusion(f32[36,12,50,50]{2,3,1,0:T(8,128)} %fusion.19), kind=kOutput, calls=%fused_computation.469 | output fusion | flops 4320049 | bytes 8726400 | tf_op jit(solution)/shard_map/sub | solution.py:79
  156.8 10.7 convert_bitcast_fusion
  167.6 4.2 copy.157
  171.7 10.1 convert_element_type.396
  181.9 4.7 fusion.242
  189.0 27.1 %fusion.243 = (f32[1800]{0:T(1024)S(1)}, f32[1800,768]{1,0:T(8,128)}) fusion(f32[768]{0:T(1024)S(1)} %convert_element_type.403, f32[1800,768]{1,0:T(8,128)} %copy-done.45, bf16[3072,768]{1,0:T(8,128)(2,1)} %param.59, bf16[768,3072]{1,0:T(8,128)(2,1)} %param.57, f32[3072]{0:T(1024)S(1)} %convert_element_type.401, f32[768]{0:T(1024)S(1)} %convert_element_type.399, ...), kind=kOutput, calls=%fused_computation.471 | convolution fusion | flops 17053284352 | bytes 20539488 | tf_op jit(solution)/shard_map/dot_general | solution.py:19
  216.1 3.5 multiply_reduce_fusion.1
  220.3 3.1 multiply_add_fusion
  223.4 6.9 reshape.525
  230.4 3.5 reduce_sum.882
  235.5 3.9 convolution_convert_fusion.3
  239.4 2.9 reshape.518
  250.9 2.9 convolution_convert_fusion.1
  253.9 2.7 reshape.522
  256.6 3.5 fusion.230
  260.1 3.2 fusion.232
  272.7 3.9 convolution_convert_fusion.2
  276.6 4.1 reshape.520
  280.7 3.4 fusion.229
  284.0 3.8 fusion.234
  296.6 4.9 convolution_add_fusion.2
  301.6 4.8 fusion.240
  316.1 2.4 multiply_reduce_fusion.30
  339.6 50.8 %all-gather.27.cloned.1.call-done = bf16[32,36,768]{2,1,0:T(8,128)(2,1)} async-done(((bf16[1,36,768]{2,1,0:T(8,128)(2,1)}), bf16[32,36,768]{2,1,0:T(8,128)(2,1)}) %all-gather.27.cloned.1.call-update) | async-done | bytes 1769488 | tf_op jit(solution)/shard_map/all_gather | solution.py:324
  390.4 3.6 reshape.554
  394.0 3.5 multiply_reduce_fusion.22
  397.5 38.7 %psum.119 = f32[1152]{0:T(1024)} all-reduce(f32[1152]{0:T(1024)} %get-tuple-element.53), channel_id=1, replica_groups=mesh['dp'=16,'fsdp'=2] {'dp','fsdp'}, use_global_device_ids=true, to_apply=%region_42.0 | all-reduce | flops 1152 | bytes 9216 | tf_op jit(solution)/shard_map/psum | solution.py:316
  458.0 6.5 fusion.244
  464.5 5.9 fusion.245
  473.2 4.2 fusion.246
  479.4 3.4 multiply_reduce_fusion.6
  486.7 3.8 fusion.225
  495.7 2.4 multiply_reduce_fusion.3
  503.4 4.1 convert_element_type.433
  508.7 3.3 fusion.222
  529.7 4.3 convert_element_type.419
  543.7 3.3 convert_element_type.426
  547.0 2.7 fusion.211
  551.1 4.2 add_add_fusion.2
  556.4 3.8 fusion.208
  562.3 8.0 add_add_fusion
  574.8 5.2 add_add_fusion.1
  580.1 66.3 %reduce-scatter.6.cloned.1.call-done = f32[384,2304]{1,0:T(8,128)} async-done(((f32[768,2304]{1,0:T(8,128)}), f32[384,2304]{1,0:T(8,128)}) %reduce-scatter.6.cloned.1.call-update) | async-done | bytes 3538960 | tf_op jit(solution)/shard_map/reduce_scatter | solution.py:369
  646.5 112.9 %reduce-scatter.12.cloned.1.call-done = f32[1536,768]{1,0:T(8,128)} async-done(((f32[3072,768]{1,0:T(8,128)}), f32[1536,768]{1,0:T(8,128)}) %reduce-scatter.12.cloned.1.call-update) | async-done | bytes 4718608 | tf_op jit(solution)/shard_map/reduce_scatter | solution.py:376
  759.3 113.0 %reduce-scatter.10.cloned.1.call-done = f32[384,3072]{1,0:T(8,128)} async-done(((f32[768,3072]{1,0:T(8,128)}), f32[384,3072]{1,0:T(8,128)}) %reduce-scatter.10.cloned.1.call-update) | async-done | bytes 4718608 | tf_op jit(solution)/shard_map/reduce_scatter | solution.py:374
  878.2 42.8 %all-reduce.9 = (f32[1]{0:T(128)}, f32[1]{0:T(128)}) all-reduce(f32[1]{0:T(128)} %bitcast.43, f32[1]{0:T(128)} %bitcast.44), channel_id=1, replica_groups=mesh['dp'=16,'fsdp'=2] {'dp','fsdp'}, use_global_device_ids=true, to_apply=%region_148.0 | all-reduce | flops 2 | bytes 16 | tf_op jit(solution)/shard_map/psum | solution.py:337
  921.2 3.5 fusion.247
  930.6 9.6 all-reduce.12
  940.9 60.8 %all-reduce.10 = (f32[384]{0:T(512)}, f32[384]{0:T(512)}, f32[384]{0:T(512)}, f32[384]{0:T(512)}, f32[384]{0:T(512)}, /*index=5*/f32[1536]{0:T(1024)}, f32[384]{0:T(512)}, f32[384]{0:T(512)}, f32[384]{0:T(512)}) all-reduce(f32[384]{0:T(512)S(1)} %dynamic-slice.1, f32[384]{0:T(512)S(1)} %dynamic-slice.3, ...), channel_id=1, replica_groups=mesh['dp'=16,'fsdp'=2] {'dp'}, use_global_device_ids=true, to_apply=%region_68.0 | all-reduce | flops 4608 | bytes 36864 | tf_op jit(solution)/shard_map/psum | solution.py:387
  1004.8 152.5 %all-reduce.15.cloned.1.call-done = (f32[384,2304]{1,0:T(8,128)}, f32[384,768]{1,0:T(8,128)}, f32[384,3072]{1,0:T(8,128)}, f32[1536,768]{1,0:T(8,128)}, f32[384,768]{1,0:T(8,128)}) async-done(((f32[384,2304]{1,0:T(8,128)}, f32[384,768]{1,0:T(8,128)}, f32[384,3072]{1,0:T(8,128)}, f32[1536,768]{1,0:T(8,128)}, f32[384,768]{1,0:T(8,128)}), (f32[384,2304]{1,0:T(8,128)}, f32[384,768]{1,0:T(8,128)}, ...) | async-done | bytes 15335440 | tf_op jit(solution)/shard_map/psum | solution.py:387
  1157.3 4.2 copy.290
  (728 shorter events, 186.9 us)
Async XLA Ops:
  7.2 69.9 %copy-start = (bf16[768,2304]{1,0:T(8,128)(2,1)S(1)}, bf16[768,2304]{1,0:T(8,128)(2,1)}, u32[]{:S(2)}) copy-start(bf16[768,2304]{1,0:T(8,128)(2,1)} %param.52) | copy-start | bytes 10616836
  7.2 228.3 %all-gather.17.cloned.1.call-start = ((), (), s32[]{:S(2)}) async-start(), calls=%async_computation.5 | async-start | bytes 5308416 | tf_op jit(solution)/shard_map/all_gather | solution.py:344
  7.9 240.4 %all-gather.19.cloned.1.call-start = ((), (), s32[]{:S(2)}) async-start(), calls=%async_computation.6 | async-start | bytes 1769472 | tf_op jit(solution)/shard_map/all_gather | solution.py:294
  8.7 287.9 %all-gather.21.cloned.1.call-start = ((), (), s32[]{:S(2)}) async-start(), calls=%async_computation.7 | async-start | bytes 7077888 | tf_op jit(solution)/shard_map/all_gather | solution.py:298
  9.4 5.3 copy-start.223
  9.4 10.6 copy-start.224
  9.4 292.1 %all-gather.23.cloned.1.call-start = ((), (), s32[]{:S(2)}) async-start(), calls=%async_computation.8 | async-start | bytes 7077888 | tf_op jit(solution)/shard_map/all_gather | solution.py:300
  10.0 306.1 %all-gather.25.cloned.1.call-start = ((), (), s32[]{:S(2)}) async-start(), calls=%async_computation.9 | async-start | bytes 1769472 | tf_op jit(solution)/shard_map/all_gather | solution.py:304
  10.6 379.8 %all-gather.27.cloned.1.call-start = ((), (), s32[]{:S(2)}) async-start(), calls=%async_computation.15 | async-start | bytes 2027520 | tf_op jit(solution)/shard_map/all_gather | solution.py:324
  12.0 223.5 %copy-start.132 = (f32[192]{0:T(256)}, f32[192]{0:T(256)S(1)}, u32[]{:S(2)}) copy-start(f32[192]{0:T(256)S(1)} %broadcast_multiply_fusion.11) | copy-start | bytes 2308
  12.0 8.0 copy-start.134
  12.1 7.9 copy-start.138
  14.2 5.8 copy-start.183
  30.7 238.5 %copy-start.113 = (f32[768]{0:T(1024)}, f32[768]{0:T(1024)S(1)}, u32[]{:S(2)}) copy-start(f32[768]{0:T(1024)S(1)} %reshape.557) | copy-start | bytes 9220
  171.7 10.1 copy-start.217
  171.7 10.1 copy-start.20
  230.3 5.2 copy-start.5
  230.4 5.1 copy-start.151
  250.1 51.5 %copy-start.7 = (f32[192,768]{1,0:T(8,128)}, f32[192,768]{1,0:T(8,128)S(1)}, u32[]{:S(2)}) copy-start(f32[192,768]{1,0:T(8,128)S(1)} %get-tuple-element.156) | copy-start | bytes 1769476
  266.9 5.8 copy-start.139
  270.7 5.8 copy-start.11
  290.8 5.8 copy-start.62
  290.8 5.8 copy-start.63
  294.6 16.2 %copy-start.9 = (f32[192,768]{1,0:T(8,128)}, f32[192,768]{1,0:T(8,128)S(1)}, u32[]{:S(2)}) copy-start(f32[192,768]{1,0:T(8,128)S(1)} %get-tuple-element.148) | copy-start | bytes 1769476
  301.6 6.1 slice-start.4
  306.4 7.5 copy-start.32
  306.5 7.4 copy-start.142
  316.1 10.4 copy-start.4
  332.0 248.1 %reduce-scatter.14.cloned.1.call-start = ((), (), s32[]{:S(2)}) async-start(), calls=%async_computation.14 | async-start | bytes 3538944 | tf_op jit(solution)/shard_map/reduce_scatter | solution.py:380
  436.2 5.3 copy-start.226
  436.2 5.3 copy-start.228
  436.2 5.3 copy-start.230
  436.2 5.3 copy-start.84
  436.2 5.3 copy-start.85
  436.2 5.3 copy-start.87
  436.2 5.3 copy-start.211
  436.3 5.3 copy-start.212
  436.3 5.3 copy-start.214
  436.3 5.4 copy-start.97
  437.1 6.6 copy-start.111
  451.3 13.2 %copy-start.24 = (f32[192,768]{1,0:T(8,128)}, f32[192,768]{1,0:T(8,128)S(1)}, u32[]{:S(2)}) copy-start(f32[192,768]{1,0:T(8,128)S(1)} %get-tuple-element.136) | copy-start | bytes 1769476
  451.3 21.8 %copy-start.26 = (f32[192,768]{1,0:T(8,128)}, f32[192,768]{1,0:T(8,128)S(1)}, u32[]{:S(2)}) copy-start(f32[192,768]{1,0:T(8,128)S(1)} %get-tuple-element.135) | copy-start | bytes 1769476
  457.9 15.2 %copy-start.199 = (f32[192]{0:T(256)}, f32[192]{0:T(256)S(1)}, u32[]{:S(2)}) copy-start(f32[192]{0:T(256)S(1)} %negate_multiply_fusion.6) | copy-start | bytes 2308
  458.0 6.5 copy-start.15
  458.0 6.5 copy-start.197
  458.0 13.5 %slice-start = ((s8[4718592]{0:T(1024)(128)(4,1)}), s8[4194304]{0:T(1024)(128)(4,1)S(1)}, s32[]{:S(2)}) async-start(s8[4718592]{0:T(1024)(128)(4,1)} %bitcast.231), calls=%async_computation.17 | async-start | bytes 8388608
  458.0 15.2 %slice-start.6 = ((s8[4718592]{0:T(1024)(128)(4,1)}), s8[4194304]{0:T(1024)(128)(4,1)S(1)}, s32[]{:S(2)}) async-start(s8[4718592]{0:T(1024)(128)(4,1)} %bitcast.244), calls=%async_computation.23 | async-start | bytes 8388608
  464.5 14.7 %copy-start.71 = (bf16[192,3072]{1,0:T(8,128)(2,1)}, bf16[192,3072]{1,0:T(8,128)(2,1)S(1)}, u32[]{:S(2)}) copy-start(bf16[192,3072]{1,0:T(8,128)(2,1)S(1)} %get-tuple-element.184) | copy-start | bytes 3538948
  464.5 7.0 slice-start.1
  464.5 8.7 slice-start.7
  473.2 6.0 copy-start.94
  485.9 94.2 %reduce-scatter.8.cloned.1.call-start = ((), (), s32[]{:S(2)}) async-start(), calls=%async_computation.11 | async-start | bytes 3538944 | tf_op jit(solution)/shard_map/reduce_scatter | solution.py:370
  521.3 125.2 %reduce-scatter.6.cloned.1.call-start = ((), (), s32[]{:S(2)}) async-start(), calls=%async_computation.10 | async-start | bytes 10616832 | tf_op jit(solution)/shard_map/reduce_scatter | solution.py:369
  555.4 204.0 %reduce-scatter.12.cloned.1.call-start = ((), (), s32[]{:S(2)}) async-start(), calls=%async_computation.13 | async-start | bytes 14155776 | tf_op jit(solution)/shard_map/reduce_scatter | solution.py:376
  570.3 302.0 %reduce-scatter.10.cloned.1.call-start = ((), (), s32[]{:S(2)}) async-start(), calls=%async_computation.12 | async-start | bytes 14155776 | tf_op jit(solution)/shard_map/reduce_scatter | solution.py:374
  580.0 577.3 %all-reduce.15.cloned.1.call-start = ((), (), s32[]{:S(2)}) async-start(), calls=%async_computation.16 | async-start | bytes 30670848 | tf_op jit(solution)/shard_map/psum | solution.py:387
  872.4 48.6 %copy-start.70 = (f32[12,768]{1,0:T(8,128)S(1)}, f32[12,768]{1,0:T(8,128)}, u32[]{:S(2)}) copy-start(f32[12,768]{1,0:T(8,128)} %copy-done.69) | copy-start | bytes 110596
  872.4 48.7 %copy-start.66 = (f32[12,768]{1,0:T(8,128)S(1)}, f32[12,768]{1,0:T(8,128)}, u32[]{:S(2)}) copy-start(f32[12,768]{1,0:T(8,128)} %copy-done.65) | copy-start | bytes 110596
  872.4 48.7 %copy-start.68 = (f32[12,768]{1,0:T(8,128)S(1)}, f32[12,768]{1,0:T(8,128)}, u32[]{:S(2)}) copy-start(f32[12,768]{1,0:T(8,128)} %copy-done.67) | copy-start | bytes 110596
  872.4 48.8 %copy-start.44 = (bf16[192,2304]{1,0:T(8,128)(2,1)S(1)}, bf16[192,2304]{1,0:T(8,128)(2,1)}, u32[]{:S(2)}) copy-start(bf16[192,2304]{1,0:T(8,128)(2,1)} %copy-done.43) | copy-start | bytes 2654212
  928.8 72.9 %copy-start.60 = (f32[192,768]{1,0:T(8,128)}, f32[192,768]{1,0:T(8,128)S(1)}, u32[]{:S(2)}) copy-start(f32[192,768]{1,0:T(8,128)S(1)} %get-tuple-element.182) | copy-start | bytes 1769476
  928.9 72.8 %copy-start.23 = (f32[192,768]{1,0:T(8,128)S(1)}, f32[192,768]{1,0:T(8,128)}, u32[]{:S(2)}) copy-start(f32[192,768]{1,0:T(8,128)} %copy-done.22) | copy-start | bytes 1769476
  928.9 72.8 %copy-start.40 = (f32[192,768]{1,0:T(8,128)S(1)}, f32[192,768]{1,0:T(8,128)}, u32[]{:S(2)}) copy-start(f32[192,768]{1,0:T(8,128)} %copy-done.38) | copy-start | bytes 1769476
  1157.3 5.2 copy-start.46
  (188 other events, 445.2 us)
Sparse Core Ops, SparseCore 0:
  9.6 52.3 all-gather.16
  63.5 22.7 all-gather.18
  87.9 62.6 all-gather.20
  152.0 62.6 all-gather.22
  216.1 22.7 all-gather.24
  332.1 58.1 all-gather.26
  486.0 35.3 reduce-scatter.13
  523.8 34.6 reduce-scatter.7
  560.9 85.5 reduce-scatter.5
  648.7 110.5 reduce-scatter.11
  761.7 110.5 reduce-scatter.9
  878.0 279.2 all-reduce.14
where the time goes:
time: 1190 us; the launch traced here: 1180 us
  waiting for transfers between devices  499 us (42%)
  matrix products  208 us (17%)
  blocking collectives  192 us (16%)
  local copies, waits for them, and re-layouts  162 us (14%)
  other arithmetic  92.4 us (8%)
  between operations  23.7 us (2%)
    psum x1, waiting for transfers between devices, on_device(): lax.psum((shard_grads[0], shard_grads[1], shard_grads[2], shard_grads[3],...  153 us
    reduce_scatter x1, waiting for transfers between devices, on_device(): lax.psum_scatter(grad_terms[7], 'fsdp', scatter_dimension=0, tiled=True)  113 us
    reduce_scatter x1, waiting for transfers between devices, on_device(): lax.psum_scatter(grad_terms[9], 'fsdp', scatter_dimension=0, tiled=True)  113 us
    dot_general x20, matrix products, product(): return jnp.dot(left_side, right_side, preferred_element_type=jnp.float32)  81.3 us
    reduce_scatter x1, waiting for transfers between devices, on_device(): lax.psum_scatter(grad_terms[2], 'fsdp', scatter_dimension=0, tiled=True)  66.3 us
    psum x1, blocking collectives, on_device(): lax.psum((shard_grads[0], shard_grads[1], shard_grads[2], shard_grads[3],...  60.8 us
    all_gather x1, waiting for transfers between devices, on_device(): shard_piece = lax.all_gather(image_low, ('dp', 'fsdp'), axis=0, tiled=True)  50.8 us
    psum x1, blocking collectives, on_device(): lax.psum((loss_part, temper * temper_grad), ('dp', 'fsdp'))  42.8 us
  transfers between devices with their start and end apart: 12, of which 5 were waited for; matrix products, arithmetic and copies ran while one was open for 31% of the time, Pallas kernels for 0%

commit v1 on v0

--- a/solution.py
+++ b/solution.py
@@ -1,14 +1,16 @@
+import functools
+
 import jax
 import jax.numpy as jnp
 from jax import lax
+from jax.experimental import pallas as pl
+from jax.experimental.pallas import tpu as pltpu
 from jax.sharding import PartitionSpec as P
 
 HEADS = 12
 HEAD_DIM = 64
 TEXT_LEN = 16
 IMAGE_LEN = 50
-PER_BATCH = 12
-BATCHES = 3
 SLOTS = 36
 
 
@@ -144,7 +146,6 @@
     factor = HEAD_DIM ** (-0.5)
     unused_unit, norm_back = jax.vjp(normalize, embedding)
     embed_grad = norm_back(unit_grad)[0].astype(jnp.bfloat16)
-    project_grad = contract_first(pooled.astype(jnp.bfloat16), embed_grad)
     pooled_grad = contract_last(embed_grad, projection)
     final_grad = jnp.broadcast_to(
         pooled_grad[:, None, :] / length, (seq_count, length, model_width)
@@ -155,13 +156,11 @@
     output_grad, endgain_grad, endoffset_grad = end_back(final_grad)
     down_low = output_grad.astype(jnp.bfloat16)
     downbias_grad = jnp.sum(output_grad, axis=0)
-    downward_grad = contract_first(active, down_low)
     active_grad = contract_last(down_low, down_weight)
     unused_active, gelu_back = jax.vjp(jax.nn.gelu, pre_active)
     pre_grad = gelu_back(active_grad)[0]
     upbias_grad = jnp.sum(pre_grad, axis=0)
     pre_low = pre_grad.astype(jnp.bfloat16)
-    upward_grad = contract_first(normed_two, pre_low)
     normed_grad = contract_last(pre_low, up_weight)
     unused_feed, feed_back = jax.vjp(
         layer_norm, residual, feed_gain.astype(jnp.float32), feed_offset.astype(jnp.float32)
@@ -170,7 +169,6 @@
     residual_grad = output_grad + residual_part
     mixbias_grad = jnp.sum(residual_grad, axis=0)
     mix_low = residual_grad.astype(jnp.bfloat16)
-    mixer_grad = contract_first(attended, mix_low)
     attended_grad = contract_last(mix_low, mixer_weight).astype(jnp.bfloat16)
     attended_grad = attended_grad.reshape(seq_count, length, HEADS, HEAD_DIM)
     queries = triple[:, :, 0]
@@ -196,30 +194,472 @@
     )
     triple_grad = jnp.stack([query_grad, key_grad, value_grad], axis=2)
     triple_grad = triple_grad.reshape(total_rows, 3 * model_width).astype(jnp.bfloat16)
-    joint_grad = contract_first(normed, triple_grad)
     first_grad = contract_last(triple_grad, joint_weight)
     unused_first, first_back = jax.vjp(
         layer_norm, inputs, norm_gain.astype(jnp.float32), norm_offset.astype(jnp.float32)
     )
     input_part, gain_grad, offset_grad = first_back(first_grad)
     input_grad = residual_grad + input_part
-    grad_terms = (
+    factors = (
+        (normed, triple_grad),
+        (attended, mix_low),
+        (normed_two, pre_low),
+        (active, down_low),
+        (pooled.astype(jnp.bfloat16), embed_grad),
+    )
+    vectors = (
         gain_grad,
         offset_grad,
-        joint_grad,
-        mixer_grad,
         mixbias_grad,
         feedgain_grad,
         feedoffset_grad,
-        upward_grad,
         upbias_grad,
-        downward_grad,
         downbias_grad,
         endgain_grad,
         endoffset_grad,
-        project_grad,
-    )
-    return (grad_terms, input_grad)
+    )
+    return (factors, vectors, input_grad)
+
+
+WIDTH = 768
+HALF = 384
+QUARTER = 192
+SUB = 2
+ROWS = QUARTER // SUB
+PART = ROWS // 2
+UNITS = 13
+STEPS = UNITS * SUB
+FACTOR_A = 8
+FACTOR_B = 10
+VECTOR_ROWS = 16
+MESH = pl.DeviceIdType.MESH
+
+
+def factor_a(unit):
+    return jnp.minimum(unit, 4) + jnp.clip(unit - 7, 0, 2) + jnp.maximum(unit - 11, 0)
+
+
+def factor_b(unit):
+    return jnp.maximum(unit - 3, 0)
+
+
+def reduce_body(
+    a_hbm,
+    b_hbm,
+    vector_ref,
+    grad_hbm,
+    vector_out,
+    a_vmem,
+    b_vmem,
+    core_out,
+    part,
+    core_in,
+    x_in,
+    y_in,
+    end_in,
+    mid_in,
+    total,
+    vector_core,
+    vector_x,
+    vector_y,
+    vector_z,
+    vector_sum,
+    a_sem,
+    b_sem,
+    core_sems,
+    x_sems,
+    y_sems,
+    end_sems,
+    mid_sems,
+    back_sems,
+    wide_sems,
+    twin_sems,
+    out_sem,
+    vector_sems,
+):
+    dp = lax.axis_index("dp")
+    x = lax.axis_index("fsdp")
+    z = dp // 4
+    y = (dp // 2) % 2
+    core = dp % 2
+    at_end = (z == 0) | (z == 3)
+    at_mid = (z == 1) | (z == 2)
+    z_pair = z + 1 - 2 * (z % 2)
+    core_peer = (dp + 1 - 2 * core, x)
+    x_peer = (dp, 1 - x)
+    y_peer = (dp + 2 - 4 * y, x)
+    pair_peer = (z_pair * 4 + y * 2 + core, x)
+    mid_peer = ((3 - z) * 4 + y * 2 + core, x)
+
+    a_copies = [pltpu.make_async_copy(a_hbm.at[k], a_vmem.at[k], a_sem.at[k]) for k in range(FACTOR_A)]
+    b_copies = [pltpu.make_async_copy(b_hbm.at[k], b_vmem.at[k], b_sem.at[k]) for k in range(FACTOR_B)]
+    for unit in range(UNITS):
+        if unit < 5 or unit in (8, 9, 12):
+            a_copies[min(unit, 4) + min(max(unit - 7, 0), 2) + max(unit - 11, 0)].start()
+        if unit == 0 or unit >= 4:
+            b_copies[max(unit - 3, 0)].start()
+
+    barrier = pltpu.get_barrier_semaphore()
+    for peer in (core_peer, x_peer, y_peer):
+        pl.semaphore_signal(barrier, inc=1, device_id=peer, device_id_type=MESH)
+    for step in range(1, 4):
+        other = ((z + step) % 4) * 4 + y * 2 + core
+        pl.semaphore_signal(barrier, inc=1, device_id=(other, x), device_id_type=MESH)
+    pl.semaphore_wait(barrier, 6)
+
+    def remote(source, target, sems, index, peer):
+        return pltpu.make_async_remote_copy(
+            src_ref=source,
+            dst_ref=target,
+            send_sem=sems.at[0, index],
+            recv_sem=sems.at[1, index],
+            device_id=peer,
+            device_id_type=MESH,
+        )
+
+    def core_copy(step):
+        return remote(core_out.at[step % 2], core_in.at[step], core_sems, step, core_peer)
+
+    def x_copy(step):
+        return remote(part.at[step, 1 - x], x_in.at[step], x_sems, step, x_peer)
+
+    def y_copy(step):
+        rows = pl.ds(pl.multiple_of((1 - y) * PART, PART), PART)
+        return remote(part.at[step, x, rows], y_in.at[step], y_sems, step, y_peer)
+
+    def own_rows():
+        return pl.ds(pl.multiple_of(y * PART, PART), PART)
+
+    def end_copy(step):
+        return remote(part.at[step, x, own_rows()], end_in.at[step], end_sems, step, pair_peer)
+
+    def mid_copy(step):
+        return remote(part.at[step, x, own_rows()], mid_in.at[step], mid_sems, step, mid_peer)
+
+    def total_rows(step):
+        return pl.ds(pl.multiple_of(y * PART, PART), PART)
+
+    def back_copy(step):
+        piece = total.at[step, core, total_rows(step)]
+        return remote(piece, piece, back_sems, step, pair_peer)
+
+    def wide_copy(step):
+        piece = total.at[step, core, total_rows(step)]
+        return remote(piece, piece, wide_sems, step, y_peer)
+
+    def twin_copy(step):
+        piece = total.at[step, core]
+        return remote(piece, piece, twin_sems, step, core_peer)
+
+    def out_copy(step, which):
+        unit = step // SUB
+        offset = pl.multiple_of(which * QUARTER + (step % SUB) * ROWS, ROWS)
+        return pltpu.make_async_copy(
+            total.at[step, which], grad_hbm.at[unit, pl.ds(offset, ROWS)], out_sem.at[step, which]
+        )
+
+    vector_first = remote(vector_ref, vector_core, vector_sems, 0, core_peer)
+    vector_second = remote(vector_sum.at[0], vector_x, vector_sems, 1, x_peer)
+    vector_third = remote(vector_sum.at[1], vector_y, vector_sems, 2, y_peer)
+    vector_last = []
+    for step in range(1, 4):
+        other = ((z + step) % 4) * 4 + y * 2 + core
+        vector_last.append(
+            remote(vector_sum.at[2], vector_z.at[step - 1], vector_sems, 2 + step, (other, x))
+        )
+
+    def wide(values):
+        return values.astype(jnp.float32)
+
+    def low(values):
+        return values.astype(jnp.bfloat16)
+
+    @pl.loop(0, STEPS + 8)
+    def _(time):
+        @pl.when((time >= 1) & (time - 1 < STEPS))
+        def _():
+            step = time - 1
+            core_copy(step).wait()
+            part[step, 1 - x] = low(wide(part[step, 1 - x]) + wide(core_in[step, 1 - x]))
+            x_copy(step).start()
+            part[step, x] = low(wide(part[step, x]) + wide(core_in[step, x]))
+
+        @pl.when(time < STEPS)
+        def _():
+            step = time
+            unit = step // SUB
+            half = step % SUB
+            slot_a = factor_a(unit)
+            slot_b = factor_b(unit)
+
+            @pl.when((half == 0) & ((unit < 5) | (unit == 8) | (unit == 9) | (unit == 12)))
+            def _():
+                pltpu.make_async_copy(a_hbm.at[slot_a], a_vmem.at[slot_a], a_sem.at[slot_a]).wait()
+
+            @pl.when((half == 0) & ((unit == 0) | (unit >= 4)))
+            def _():
+                pltpu.make_async_copy(b_hbm.at[slot_b], b_vmem.at[slot_b], b_sem.at[slot_b]).wait()
+
+            right = b_vmem[slot_b]
+            for which in range(2):
+                rows = pl.ds(
+                    pl.multiple_of(which * HALF + (1 - core) * QUARTER + half * ROWS, ROWS), ROWS
+                )
+                core_out[step % 2, which] = low(product(a_vmem[slot_a, rows], right))
+            core_copy(step).start()
+            for which in range(2):
+                rows = pl.ds(
+                    pl.multiple_of(which * HALF + core * QUARTER + half * ROWS, ROWS), ROWS
+                )
+                part[step, which] = low(product(a_vmem[slot_a, rows], right))
+
+        @pl.when((time >= 2) & (time - 2 < STEPS))
+        def _():
+            step = time - 2
+            x_copy(step).wait()
+            rows = pl.ds(pl.multiple_of((1 - y) * PART, PART), PART)
+            part[step, x, rows] = low(wide(part[step, x, rows]) + wide(x_in[step, rows]))
+            y_copy(step).start()
+            part[step, x, own_rows()] = low(
+                wide(part[step, x, own_rows()]) + wide(x_in[step, own_rows()])
+            )
+
+        @pl.when((time >= 3) & (time - 3 < STEPS))
+        def _():
+            step = time - 3
+            y_copy(step).wait()
+            part[step, x, own_rows()] = low(
+                wide(part[step, x, own_rows()]) + wide(y_in[step])
+            )
+
+            @pl.when(at_end)
+            def _():
+                end_copy(step).start()
+
+        @pl.when((time >= 4) & (time - 4 < STEPS))
+        def _():
+            step = time - 4
+
+            @pl.when(at_end)
+            def _():
+                end_copy(step).wait_send()
+
+            @pl.when(at_mid)
+            def _():
+                end_copy(step).wait_recv()
+                part[step, x, own_rows()] = low(
+                    wide(part[step, x, own_rows()]) + wide(end_in[step])
+                )
+                mid_copy(step).start()
+
+        @pl.when((time >= 5) & (time - 5 < STEPS) & at_mid)
+        def _():
+            step = time - 5
+            mid_copy(step).wait()
+            total[step, core, total_rows(step)] = low(
+                wide(part[step, x, own_rows()]) + wide(mid_in[step])
+            )
+            back_copy(step).start()
+            wide_copy(step).start()
+
+        @pl.when((time >= 6) & (time - 6 < STEPS))
+        def _():
+            step = time - 6
+
+            @pl.when(at_end)
+            def _():
+                back_copy(step).wait_recv()
+                wide_copy(step).start()
+
+            @pl.when(at_mid)
+            def _():
+                back_copy(step).wait_send()
+
+        @pl.when((time >= 7) & (time - 7 < STEPS))
+        def _():
+            step = time - 7
+            wide_copy(step).wait()
+            twin_copy(step).start()
+            out_copy(step, core).start()
+
+        @pl.when((time >= 8) & (time - 8 < STEPS))
+        def _():
+            step = time - 8
+            twin_copy(step).wait()
+            out_copy(step, 1 - core).start()
+
+        @pl.when(time == 0)
+        def _():
+            vector_first.start()
+
+        @pl.when(time == 1)
+        def _():
+            vector_first.wait()
+            vector_sum[0] = vector_ref[...] + vector_core[...]
+            vector_second.start()
+
+        @pl.when(time == 3)
+        def _():
+            vector_second.wait()
+            vector_sum[1] = vector_sum[0] + vector_x[...]
+            vector_third.start()
+
+        @pl.when(time == 5)
+        def _():
+            vector_third.wait()
+            vector_sum[2] = vector_sum[1] + vector_y[...]
+            for copy in vector_last:
+                copy.start()
+
+        @pl.when(time == 7)
+        def _():
+            for copy in vector_last:
+                copy.wait()
+            order = lax.broadcasted_iota(jnp.int32, (VECTOR_ROWS, WIDTH), 0) * 0 + z
+            own = vector_sum[2]
+            before_one = vector_z[0]
+            before_two = vector_z[1]
+            before_three = vector_z[2]
+
+            def pick(where):
+                shift = (order - where + 4) % 4
+                return jnp.where(
+                    shift == 0,
+                    own,
+                    jnp.where(
+                        shift == 1,
+                        before_one,
+                        jnp.where(shift == 2, before_two, before_three),
+                    ),
+                )
+
+            vector_out[...] = (pick(0) + pick(1)) + (pick(2) + pick(3))
+
+    @pl.loop(0, STEPS)
+    def _(step):
+        out_copy(step, core).wait()
+        out_copy(step, 1 - core).wait()
+
+
+def reduce_kernel(factors, vectors):
+    (normed, triple_grad), (attended, mix_low), (normed_two, pre_low), (active, down_low), last = (
+        factors
+    )
+    pooled, embed_grad = last
+    rows = normed.shape[0]
+    active_t = active.T.reshape(2, 4, HALF, rows).transpose(1, 0, 2, 3).reshape(4, WIDTH, rows)
+    pooled_t = jnp.pad(pooled.T, ((0, 0), (0, rows - pooled.shape[0])))
+    left = jnp.concatenate(
+        [active_t, normed_two.T[None], attended.T[None], normed.T[None], pooled_t[None]], axis=0
+    )
+    right = jnp.concatenate(
+        [
+            down_low[None],
+            pre_low.reshape(rows, 4, WIDTH).transpose(1, 0, 2),
+            mix_low[None],
+            triple_grad.reshape(rows, 3, WIDTH).transpose(1, 0, 2),
+            jnp.pad(embed_grad, ((0, rows - embed_grad.shape[0]), (0, 0)))[None],
+        ],
+        axis=0,
+    )
+    packed = jnp.concatenate([vector.reshape(-1, WIDTH) for vector in vectors], axis=0)
+    packed = jnp.pad(packed, ((0, VECTOR_ROWS - packed.shape[0]), (0, 0)))
+    any_spec = pl.BlockSpec(memory_space=pl.ANY)
+    vmem_spec = pl.BlockSpec(memory_space=pltpu.VMEM)
+    dma = pltpu.SemaphoreType.DMA
+    grads, packed = pl.pallas_call(
+        reduce_body,
+        out_shape=(
+            jax.ShapeDtypeStruct((UNITS, HALF, WIDTH), jnp.bfloat16),
+            jax.ShapeDtypeStruct((VECTOR_ROWS, WIDTH), jnp.float32),
+        ),
+        in_specs=[any_spec, any_spec, vmem_spec],
+        out_specs=(any_spec, vmem_spec),
+        scratch_shapes=[
+            pltpu.VMEM((FACTOR_A, WIDTH, rows), jnp.bfloat16),
+            pltpu.VMEM((FACTOR_B, rows, WIDTH), jnp.bfloat16),
+            pltpu.VMEM((2, 2, ROWS, WIDTH), jnp.bfloat16),
+            pltpu.VMEM((STEPS, 2, ROWS, WIDTH), jnp.bfloat16),
+            pltpu.VMEM((STEPS, 2, ROWS, WIDTH), jnp.bfloat16),
+            pltpu.VMEM((STEPS, ROWS, WIDTH), jnp.bfloat16),
+            pltpu.VMEM((STEPS, PART, WIDTH), jnp.bfloat16),
+            pltpu.VMEM((STEPS, PART, WIDTH), jnp.bfloat16),
+            pltpu.VMEM((STEPS, PART, WIDTH), jnp.bfloat16),
+            pltpu.VMEM((STEPS, 2, ROWS, WIDTH), jnp.bfloat16),
+            pltpu.VMEM((VECTOR_ROWS, WIDTH), jnp.float32),
+            pltpu.VMEM((VECTOR_ROWS, WIDTH), jnp.float32),
+            pltpu.VMEM((VECTOR_ROWS, WIDTH), jnp.float32),
+            pltpu.VMEM((3, VECTOR_ROWS, WIDTH), jnp.float32),
+            pltpu.VMEM((3, VECTOR_ROWS, WIDTH), jnp.float32),
+            dma((FACTOR_A,)),
+            dma((FACTOR_B,)),
+            dma((2, STEPS)),
+            dma((2, STEPS)),
+            dma((2, STEPS)),
+            dma((2, STEPS)),
+            dma((2, STEPS)),
+            dma((2, STEPS)),
+            dma((2, STEPS)),
+            dma((2, STEPS)),
+            dma((STEPS, 2)),
+            dma((2, 6)),
+        ],
+        compiler_params=pltpu.CompilerParams(
+            collective_id=0, has_side_effects=True, vmem_limit_bytes=62 * 1024 * 1024
+        ),
+    )(left, right, packed)
+    shard = lax.axis_index("fsdp")
+    wide = grads.astype(jnp.float32)
+
+    def matrix(first, count):
+        return wide[first : first + count].transpose(1, 0, 2).reshape(HALF, count * WIDTH)
+
+    def vector(first, count):
+        full = packed[first : first + count].reshape(2, count * HALF)
+        return lax.dynamic_index_in_dim(full, shard, 0, keepdims=False)
+
+    return (
+        vector(0, 1),
+        vector(1, 1),
+        matrix(9, 3),
+        matrix(8, 1),
+        vector(2, 1),
+        vector(3, 1),
+        vector(4, 1),
+        matrix(4, 4),
+        vector(5, 4),
+        wide[0:4].reshape(4 * HALF, WIDTH),
+        vector(9, 1),
+        vector(10, 1),
+        vector(11, 1),
+        matrix(12, 1),
+    )
+
+
+def reduce_plain(factors, vectors):
+    terms = [contract_first(left, right) for left, right in factors]
+    joint, mixer, upward, downward, project = terms
+    gain, offset, mixbias, feedgain, feedoffset, upbias, downbias, endgain, endoffset = vectors
+    ordered = (
+        gain,
+        offset,
+        joint,
+        mixer,
+        mixbias,
+        feedgain,
+        feedoffset,
+        upward,
+        upbias,
+        downward,
+        downbias,
+        endgain,
+        endoffset,
+        project,
+    )
+    shards = tuple(
+        lax.psum_scatter(term, "fsdp", scatter_dimension=0, tiled=True) for term in ordered
+    )
+    return lax.psum(shards, "dp")
 
 
 def on_device(
@@ -282,32 +722,31 @@
     text_live = lax.dynamic_slice_in_dim(live_all, device * SLOTS, SLOTS)
     temper = jnp.exp(log_scale[0])
     half_inverse = 1.0 / (2.0 * live_total)
-    batch_rows = PER_BATCH * TEXT_LEN
-    image_unit, image_kept = forward_block(image_tokens, image_weights, IMAGE_LEN)
+    image_unit = forward_block(image_tokens, image_weights, IMAGE_LEN)[0]
     image_low = image_unit.astype(jnp.bfloat16)
-    unit_list = []
-    for batch_index in range(BATCHES):
-        weights_now = (
-            lax.all_gather(text_gain, "fsdp", axis=0, tiled=True),
-            lax.all_gather(text_offset, "fsdp", axis=0, tiled=True),
-            lax.all_gather(text_joint, "fsdp", axis=0, tiled=True),
-            lax.all_gather(text_mixer, "fsdp", axis=0, tiled=True),
-            lax.all_gather(text_mixbias, "fsdp", axis=0, tiled=True),
-            lax.all_gather(text_feedgain, "fsdp", axis=0, tiled=True),
-            lax.all_gather(text_feedoffset, "fsdp", axis=0, tiled=True),
-            lax.all_gather(text_upward, "fsdp", axis=0, tiled=True),
-            lax.all_gather(text_upbias, "fsdp", axis=0, tiled=True),
-            lax.all_gather(text_downward, "fsdp", axis=0, tiled=True),
-            lax.all_gather(text_downbias, "fsdp", axis=0, tiled=True),
-            lax.all_gather(text_endgain, "fsdp", axis=0, tiled=True),
-            lax.all_gather(text_endoffset, "fsdp", axis=0, tiled=True),
-            lax.all_gather(text_project, "fsdp", axis=0, tiled=True),
+    shard_piece = lax.all_gather(image_low, ("dp", "fsdp"), axis=0, tiled=True)
+    text_weights = tuple(
+        lax.all_gather(shard, "fsdp", axis=0, tiled=True)
+        for shard in (
+            text_gain,
+            text_offset,
+            text_joint,
+            text_mixer,
+            text_mixbias,
+            text_feedgain,
+            text_feedoffset,
+            text_upward,
+            text_upbias,
+            text_downward,
+            text_downbias,
+            text_endgain,
+            text_endoffset,
+            text_project,
         )
-        batch_tokens = text_tokens[batch_index * batch_rows : (batch_index + 1) * batch_rows]
-        unit_list.append(forward_block(batch_tokens, weights_now, TEXT_LEN)[0])
-    text_unit = jnp.concatenate(unit_list, axis=0)
+    )
+    text_unit, kept_values = forward_block(text_tokens, text_weights, TEXT_LEN)
     text_low = text_unit.astype(jnp.bfloat16)
-    cosine = contract_last(text_low, lax.all_gather(image_low, ("dp", "fsdp"), axis=0, tiled=True))
+    cosine = contract_last(text_low, shard_piece)
     scaled = jnp.exp(temper * cosine - temper)
     image_live = live_all
     forward_row_sum = jnp.sum(scaled * image_live[None, :], axis=1)
@@ -321,10 +760,6 @@
     loss_part = jnp.sum(text_live * (row_log - diagonal) + text_live * (column_log - diagonal)) / (
         2.0 * live_total
     )
-    shard_piece = lax.all_gather(image_low, ("dp", "fsdp"), axis=0, tiled=True)
-    cosine = contract_last(text_low, shard_piece)
-    scaled = jnp.exp(temper * cosine - temper)
-    image_live = live_all
     coupling = (
         scaled * (text_live / forward_row_sum)[:, None] * image_live[None, :]
         + scaled * text_live[:, None] * (image_live / column_sum)[None, :]
@@ -335,90 +770,15 @@
     unit_grad = unit_grad - temper / live_total * text_live[:, None] * image_low.astype(jnp.float32)
     temper_grad = temper_grad - jnp.sum(text_live * diagonal_cos) / live_total
     loss_total, scale_total = lax.psum((loss_part, temper * temper_grad), ("dp", "fsdp"))
-    input_list = []
-    shard_grads = None
-    for batch_index in range(BATCHES):
-        weights_now = (
-            lax.all_gather(text_gain, "fsdp", axis=0, tiled=True),
-            lax.all_gather(text_offset, "fsdp", axis=0, tiled=True),
-            lax.all_gather(text_joint, "fsdp", axis=0, tiled=True),
-            lax.all_gather(text_mixer, "fsdp", axis=0, tiled=True),
-            lax.all_gather(text_mixbias, "fsdp", axis=0, tiled=True),
-            lax.all_gather(text_feedgain, "fsdp", axis=0, tiled=True),
-            lax.all_gather(text_feedoffset, "fsdp", axis=0, tiled=True),
-            lax.all_gather(text_upward, "fsdp", axis=0, tiled=True),
-            lax.all_gather(text_upbias, "fsdp", axis=0, tiled=True),
-            lax.all_gather(text_downward, "fsdp", axis=0, tiled=True),
-            lax.all_gather(text_downbias, "fsdp", axis=0, tiled=True),
-            lax.all_gather(text_endgain, "fsdp", axis=0, tiled=True),
-            lax.all_gather(text_endoffset, "fsdp", axis=0, tiled=True),
-            lax.all_gather(text_project, "fsdp", axis=0, tiled=True),
-        )
-        batch_tokens = text_tokens[batch_index * batch_rows : (batch_index + 1) * batch_rows]
-        unit_now, kept_values = forward_block(batch_tokens, weights_now, TEXT_LEN)
-        grad_terms, input_grad = backward_block(
-            kept_values,
-            weights_now,
-            unit_grad[batch_index * PER_BATCH : (batch_index + 1) * PER_BATCH],
-            TEXT_LEN,
-        )
-        input_list.append(input_grad)
-        batch_shards = (
-            lax.psum_scatter(grad_terms[0], "fsdp", scatter_dimension=0, tiled=True),
-            lax.psum_scatter(grad_terms[1], "fsdp", scatter_dimension=0, tiled=True),
-            lax.psum_scatter(grad_terms[2], "fsdp", scatter_dimension=0, tiled=True),
-            lax.psum_scatter(grad_terms[3], "fsdp", scatter_dimension=0, tiled=True),
-            lax.psum_scatter(grad_terms[4], "fsdp", scatter_dimension=0, tiled=True),
-            lax.psum_scatter(grad_terms[5], "fsdp", scatter_dimension=0, tiled=True),
-            lax.psum_scatter(grad_terms[6], "fsdp", scatter_dimension=0, tiled=True),
-            lax.psum_scatter(grad_terms[7], "fsdp", scatter_dimension=0, tiled=True),
-            lax.psum_scatter(grad_terms[8], "fsdp", scatter_dimension=0, tiled=True),
-            lax.psum_scatter(grad_terms[9], "fsdp", scatter_dimension=0, tiled=True),
-            lax.psum_scatter(grad_terms[10], "fsdp", scatter_dimension=0, tiled=True),
-            lax.psum_scatter(grad_terms[11], "fsdp", scatter_dimension=0, tiled=True),
-            lax.psum_scatter(grad_terms[12], "fsdp", scatter_dimension=0, tiled=True),
-            lax.psum_scatter(grad_terms[13], "fsdp", scatter_dimension=0, tiled=True),
-        )
-        shard_grads = (
-            batch_shards
-            if shard_grads is None
-            else jax.tree.map(jnp.add, shard_grads, batch_shards)
-        )
-    final_grads = lax.psum(
-        (
-            shard_grads[0],
-            shard_grads[1],
-            shard_grads[2],
-            shard_grads[3],
-            shard_grads[4],
-            shard_grads[5],
-            shard_grads[6],
-            shard_grads[7],
-            shard_grads[8],
-            shard_grads[9],
-            shard_grads[10],
-            shard_grads[11],
-            shard_grads[12],
-            shard_grads[13],
-        ),
-        "dp",
-    )
-    token_grad = jnp.concatenate(input_list, axis=0)
+    factors, vectors, token_grad = backward_block(
+        kept_values, text_weights, unit_grad, TEXT_LEN
+    )
+    if (lax.axis_size("dp"), lax.axis_size("fsdp")) == (16, 2):
+        final_grads = reduce_kernel(factors, vectors)
+    else:
+        final_grads = reduce_plain(factors, vectors)
     return (
-        final_grads[0],
-        final_grads[1],
-        final_grads[2],
-        final_grads[3],
-        final_grads[4],
-        final_grads[5],
-        final_grads[6],
-        final_grads[7],
-        final_grads[8],
-        final_grads[9],
-        final_grads[10],
-        final_grads[11],
-        final_grads[12],
-        final_grads[13],
+        *final_grads,
         jnp.reshape(scale_total, (1,)),
         token_grad,
         jnp.reshape(loss_total, (1,)),

time: 1190 us -> 863 us (0.73)
  waiting for transfers between devices: 499 us -> 164 us
  Pallas kernels: 0 us -> 120 us
  matrix products: 208 us -> 133 us
  blocking collectives: 192 us -> 118 us
  local copies, waits for them, and re-layouts: 162 us -> 214 us
    reduce_scatter x5 -> x0, waiting for transfers between devices: 292 us -> none  [the longest x1 113 us: on_device(): lax.psum_scatter(grad_terms[7], 'fsdp', scatter_dimension=0, tiled=True)]
    all_gather x5, waiting for transfers between devices: 0.03 us -> 153 us  [on_device(): lax.all_gather(shard, 'fsdp', axis=0, tiled=True)]
    psum x1 -> x0, waiting for transfers between devices: 153 us -> none  [on_device(): lax.psum((shard_grads[0], shard_grads[1], shard_grads[2], shard_grads[3],...]
    pallas_call x0 -> x1, Pallas kernels: none -> 120 us  [reduce_kernel(): pl.pallas_call(reduce_body, out_shape=(jax.ShapeDtypeStruct((UNITS, HALF,...]
    psum x1 -> x0, blocking collectives: 60.8 us -> none  [on_device(): lax.psum((shard_grads[0], shard_grads[1], shard_grads[2], shard_grads[3],...]
    all_gather x1, waiting for transfers between devices: 50.8 us -> 7.71 us  [on_device(): shard_piece = lax.all_gather(image_low, ('dp', 'fsdp'), axis=0, tiled=True)]
    dot_general x15 -> x0, matrix products: 40.1 us -> none  [contract_first(): lax.dot_general(left_side, right_side, (((0,), (0,)), ((), ())), preferre...]
    transpose x0 -> x4, local copies, waits for them, and re-layouts: none -> 20.6 us  [matrix(): wide[first:first + count].transpose(1, 0, 2).reshape(HALF, count * WIDTH)]
  transfers between devices with their start and end apart: 12 -> 6, of which waited for: 5 -> 5; matrix products, arithmetic and copies ran while one was open for 31% -> 9% of each run, Pallas kernels for 0% -> 0%
where the time goes in v1:
time: 863 us; the launch traced here: 854 us
  local copies, waits for them, and re-layouts  214 us (25%)
  waiting for transfers between devices  164 us (19%)
  matrix products  133 us (15%)
  Pallas kernels  120 us (14%)
  blocking collectives  118 us (14%)
  other arithmetic  83.2 us (10%)
  between operations  20.4 us (2%)
    all_gather x5, waiting for transfers between devices, on_device(): lax.all_gather(shard, 'fsdp', axis=0, tiled=True)  153 us
    pallas_call x1, Pallas kernels, reduce_kernel(): pl.pallas_call(reduce_body, out_shape=(jax.ShapeDtypeStruct((UNITS, HALF,...  120 us
    dot_general x10, matrix products, product(): return jnp.dot(left_side, right_side, preferred_element_type=jnp.float32)  76.3 us
    all_gather x9, blocking collectives, on_device(): lax.all_gather(shard, 'fsdp', axis=0, tiled=True)  40.2 us
    psum x1, blocking collectives, on_device(): column_sum = lax.psum(column_sum, ('dp', 'fsdp'))  39.4 us
    psum x1, blocking collectives, on_device(): lax.psum((loss_part, temper * temper_grad), ('dp', 'fsdp'))  38.5 us
    unnamed x171, local copies, waits for them, and re-layouts  37.7 us
    reshape x2, local copies, waits for them, and re-layouts, forward_block(): triple = product(normed, joint_weight).astype(jnp.bfloat16).reshape(seq_c...  34.6 us
  transfers between devices with their start and end apart: 6, of which 5 were waited for; matrix products, arithmetic and copies ran while one was open for 9% of the time, Pallas kernels for 0%

profile of v1, /device:TPU:0, one launch (start us, length us, event | category | flops | bytes accessed | tf_op | source)
XLA Modules:
  0.0 853.9 jit_solution(4286573373736505021)
XLA Ops:
  11.0 11.6 %convolution_convert_fusion = bf16[1800,2304]{1,0:T(8,128)(2,1)} fusion(bf16[768,2304]{1,0:T(8,128)(2,1)} %param.52, bf16[1800,768]{1,0:T(8,128)(2,1)S(1)} %copy-done.16, f32[768]{0:T(1024)S(1)} %convert_element_type.211, f32[768]{0:T(1024)S(1)} %convert_element_type.210, f32[1800]{0:T(1024)S(1)} %add_rsqrt_fusion.2, f32[1800]{0:T(1024)S(1)} %broadcast_multiply_fusion.2), kind=kOutput, calls=%fused_computation.13 | convolution fusion | flops 6382540800 | bytes 14618688 | tf_op jit(solution)/shard_map/dot_general | solution.py:21
  22.6 25.5 %reshape.348 = bf16[36,50,3,12,64]{4,3,2,1,0:T(8,128)(2,1)} reshape(bf16[1800,2304]{1,0:T(8,128)(2,1)} %convolution_convert_fusion) | data formatting | bytes 16588800 | tf_op jit(solution)/shard_map/reshape | solution.py:73
  48.1 15.1 %fusion.125 = (bf16[36,50,1,12,64]{4,3,2,1,0:T(8,128)(2,1)}, bf16[36,50,1,12,64]{4,3,2,1,0:T(8,128)(2,1)}, bf16[36,50,1,12,64]{4,3,2,1,0:T(8,128)(2,1)}) fusion(bf16[36,50,3,12,64]{4,3,2,1,0:T(8,128)(2,1)} %reshape.348), kind=kLoop, calls=%fused_computation.254 | loop fusion | bytes 16588800 | tf_op jit(solution)/shard_map/slice | solution.py:77
  63.2 13.1 %fusion.31 = f32[36,12,50,50]{2,3,1,0:T(8,128)} fusion(bf16[36,50,1,12,64]{4,3,2,1,0:T(8,128)(2,1)} %get-tuple-element.121, bf16[36,50,1,12,64]{4,3,2,1,0:T(8,128)(2,1)} %get-tuple-element.120), kind=kOutput, calls=%fused_computation.42 | convolution fusion | flops 138240000 | bytes 9849600 | tf_op jit(solution)/shard_map/sqhd,skhd->shqk/dot_general | solution.py:79
  76.4 16.3 %fusion.131 = (f32[36,12,50]{2,1,0:T(8,128)S(1)}, f32[36,12,50,50]{2,3,1,0:T(8,128)}) fusion(f32[36,12,50,50]{2,3,1,0:T(8,128)} %fusion.31), kind=kOutput, calls=%fused_computation.260 | output fusion | flops 4320049 | bytes 8726400 | tf_op jit(solution)/shard_map/sub | solution.py:81
  92.6 8.5 %convert_bitcast_fusion = bf16[36,50,12,64]{3,1,2,0:T(8,128)(2,1)S(1)} fusion(f32[36,12,50,50]{2,3,1,0:T(8,128)} %get-tuple-element.140, f32[36,12,50]{2,1,0:T(8,128)S(1)} %get-tuple-element.139, bf16[36,50,1,12,64]{4,3,2,1,0:T(8,128)(2,1)} %get-tuple-element.119), kind=kOutput, calls=%fused_computation.45 | convolution fusion | flops 141782400 | bytes 9936000 | tf_op jit(solution)/shard_map/shqk,skhd->sqhd/dot_general | solution.py:83
  101.2 4.2 copy.170
  105.3 10.1 %convert_element_type.217 = bf16[1800,768]{1,0:T(8,128)(2,1)} reshape(bf16[36,50,12,64]{3,2,1,0:T(8,128)(2,1)} %copy.170) | data formatting | bytes 5529600 | tf_op jit(solution)/shard_map/convert_element_type | solution.py:84
  115.5 5.2 fusion.132
  124.0 27.0 %fusion.133 = (f32[1800]{0:T(1024)S(1)}, f32[1800,768]{1,0:T(8,128)}) fusion(f32[768]{0:T(1024)S(1)} %convert_element_type.224, f32[1800,768]{1,0:T(8,128)} %copy-done.22, bf16[3072,768]{1,0:T(8,128)(2,1)} %param.59, bf16[768,3072]{1,0:T(8,128)(2,1)} %param.57, f32[3072]{0:T(1024)S(1)} %convert_element_type.222, f32[768]{0:T(1024)S(1)} %convert_element_type.220, ...), kind=kOutput, calls=%fused_computation.262 | convolution fusion | flops 17053284352 | bytes 20539488 | tf_op jit(solution)/shard_map/dot_general | solution.py:21
  151.0 3.5 multiply_reduce_fusion.1
  155.2 3.0 multiply_add_fusion
  158.3 6.4 reshape.349
  164.7 3.4 reduce_sum.394
  174.8 5.6 all-gather
  180.5 4.3 all-gather.1
  184.9 4.3 all-gather.2
  189.8 4.4 all-gather.5
  194.8 4.3 all-gather.3
  199.8 4.3 all-gather.4
  204.7 4.3 all-gather.6
  209.7 4.3 all-gather.7
  214.0 4.3 all-gather.8
  221.8 7.7 all-gather.27.cloned.1.call-done
  229.5 3.6 reshape.396
  233.1 46.1 %all-gather.17.cloned.1.call-done = bf16[768,2304]{1,0:T(8,128)(2,1)} async-done(((bf16[384,2304]{1,0:T(8,128)(2,1)}), bf16[768,2304]{1,0:T(8,128)(2,1)}) %all-gather.17.cloned.1.call-update) | async-done | bytes 3538960 | tf_op jit(solution)/shard_map/all_gather | solution.py:729
  279.3 5.9 convolution_convert_fusion.1
  285.2 9.1 %reshape.344 = bf16[36,16,3,12,64]{4,3,2,1,0:T(8,128)(2,1)} reshape(bf16[576,2304]{1,0:T(8,128)(2,1)} %convolution_convert_fusion.1) | data formatting | bytes 5308416 | tf_op jit(solution)/shard_map/reshape | solution.py:73
  294.3 4.8 fusion.127
  301.2 13.8 %fusion.128 = (f32[36,12,16]{2,1,0:T(8,128)S(1)}, f32[36,12,16,16]{2,3,1,0:T(8,128)S(1)}) fusion(f32[36,12,16,16]{2,3,1,0:T(8,128)S(1)} %fusion.73), kind=kOutput, calls=%fused_computation.257 | output fusion | flops 442383 | bytes 912384 | tf_op jit(solution)/shard_map/sub | solution.py:81
  325.0 42.8 %all-gather.21.cloned.1.call-done = bf16[768,3072]{1,0:T(8,128)(2,1)} async-done(((bf16[384,3072]{1,0:T(8,128)(2,1)}), bf16[768,3072]{1,0:T(8,128)(2,1)}) %all-gather.21.cloned.1.call-update) | async-done | bytes 4718608 | tf_op jit(solution)/shard_map/all_gather | solution.py:729
  367.7 10.5 %fusion.26 = (bf16[3072,576]{0,1:T(8,128)(2,1)}, f32[576,3072]{1,0:T(8,128)}) fusion(f32[3072]{0:T(1024)S(1)} %bitcast.143, bf16[768,3072]{1,0:T(8,128)(2,1)} %all-gather.21.cloned.1.call-done, f32[576,768]{1,0:T(8,128)S(1)} %get-tuple-element.136, f32[768]{0:T(1024)S(1)} %copy-done.42, f32[768]{0:T(1024)S(1)} %copy-done.41, f32[576]{0:T(1024)S(1)} %fusion.94, ...), kind=kOutput, calls=%fused_computation.35 | convolution fusion | flops 2737815552 | bytes 17127936 | tf_op jit(solution)/shard_map/dot_general | solution.py:21
  378.2 53.6 %all-gather.23.cloned.1.call-done = bf16[3072,768]{1,0:T(8,128)(2,1)} async-done(((bf16[1536,768]{1,0:T(8,128)(2,1)}), bf16[3072,768]{1,0:T(8,128)(2,1)}) %all-gather.23.cloned.1.call-update) | async-done | bytes 4718608 | tf_op jit(solution)/shard_map/all_gather | solution.py:729
  431.8 9.4 %fusion.130 = (f32[576]{0:T(1024)S(1)}, f32[576,768]{1,0:T(8,128)S(1)}) fusion(f32[768]{0:T(1024)S(1)} %copy-done.49, f32[576,768]{1,0:T(8,128)} %copy-done.17, bf16[3072,768]{1,0:T(8,128)(2,1)} %all-gather.23.cloned.1.call-done, f32[576,3072]{1,0:T(8,128)} %get-tuple-element.152, f32[3072]{0:T(1024)S(1)} %bitcast.144), kind=kOutput, calls=%fused_computation.259 | convolution fusion | flops 2736930304 | bytes 15353088 | tf_op jit(solution)/shard_map/dot_general | solution.py:21
  445.1 10.9 %all-gather.25.cloned.1.call-done = bf16[768,768]{1,0:T(8,128)(2,1)} async-done(((bf16[384,768]{1,0:T(8,128)(2,1)}), bf16[768,768]{1,0:T(8,128)(2,1)}) %all-gather.25.cloned.1.call-update) | async-done | bytes 1179664 | tf_op jit(solution)/shard_map/all_gather | solution.py:729
  460.6 39.4 %psum.21 = f32[1152]{0:T(1024)S(1)} all-reduce(f32[1152]{0:T(1024)S(1)} %get-tuple-element.98), channel_id=1, replica_groups=mesh['dp'=16,'fsdp'=2] {'dp','fsdp'}, use_global_device_ids=true, to_apply=%region_22.0 | all-reduce | flops 1152 | bytes 9216 | tf_op jit(solution)/shard_map/psum | solution.py:755
  510.8 10.5 %fusion.126 = (f32[3072]{0:T(1024)S(1)}, bf16[576,3072]{1,0:T(8,128)(2,1)S(1)}) fusion(f32[576,3072]{1,0:T(8,128)} %get-tuple-element.152, f32[3072]{0:T(1024)S(1)} %bitcast.145, bf16[3072,768]{1,0:T(8,128)(2,1)} %all-gather.23.cloned.1.call-done, f32[576,768]{1,0:T(8,128)} %add_add_fusion.3, f32[576]{0:T(1024)S(1)} %negate_multiply_fusion.2), kind=kOutput, calls=%fused_computation.255 | convolution fusion | flops 2757719040 | bytes 17131776 | tf_op jit(solution)/shard_map/dot_general | solution.py:25
  521.3 3.4 multiply_reduce_fusion.5
  529.9 4.1 reshape.352
  534.0 5.2 multiply_reduce_fusion.3
  548.8 4.7 copy.178
  553.5 9.5 %convert_element_type.240 = bf16[576,2304]{1,0:T(8,128)(2,1)} reshape(bf16[36,16,3,12,64]{4,3,2,1,0:T(8,128)(2,1)} %copy.178) | data formatting | bytes 5308416 | tf_op jit(solution)/shard_map/convert_element_type | solution.py:196
  562.9 5.2 fusion.68
  571.4 4.1 fusion.39
  578.7 4.1 stack.24
  582.8 3.5 copy.175
  586.3 4.1 stack.25
  590.4 3.5 copy.177
  593.8 4.1 stack.26
  597.9 3.6 fusion.57
  607.9 7.6 reshape.345
  615.4 7.7 copy.160
  623.2 4.4 constant_dynamic-update-slice_fusion.2
  631.7 120.5 %shard_map.431 = (bf16[13,384,768]{2,1,0:T(8,128)(2,1)}, f32[16,768]{1,0:T(8,128)}) custom-call(bf16[8,768,576]{2,1,0:T(8,128)(2,1)} %bitcast_dynamic-update-slice_fusion.1.a_hbm, bf16[10,576,768]{2,1,0:T(8,128)(2,1)} %bitcast_dynamic-update-slice_fusion.2.b_hbm, f32[16,768]{1,0:T(8,128)} %pad.14.vector_ref), custom_call_target="tpu_custom_call" | custom-call | tf_op jit(solution)/shard_map/pallas_call | solution.py:570
  752.2 10.1 %convert_element_type.241 = f32[13,384,768]{2,1,0:T(8,128)} convert(bf16[13,384,768]{2,1,0:T(8,128)(2,1)} %get-tuple-element.20) | non-fusion elementwise | flops 3833856 | bytes 23003136 | tf_op jit(solution)/shard_map/convert_element_type | solution.py:612
  762.3 5.0 slice_bitcast_fusion
  767.3 4.2 slice_bitcast_fusion.1
  771.5 3.2 slice_bitcast_fusion.2
  774.7 2.6 slice.92
  780.0 6.3 copy.180
  786.3 6.0 copy.182
  792.4 5.2 copy.179
  797.5 5.2 copy.181
  808.3 38.5 %all-reduce.3 = (f32[1]{0:T(128)}, f32[1]{0:T(128)}) all-reduce(f32[1]{0:T(128)} %bitcast.42, f32[1]{0:T(128)} %bitcast.43), channel_id=1, replica_groups=mesh['dp'=16,'fsdp'=2] {'dp','fsdp'}, use_global_device_ids=true, to_apply=%region_42.0 | all-reduce | flops 2 | bytes 16 | tf_op jit(solution)/shard_map/psum | solution.py:772
  (312 shorter events, 86.8 us)
Async XLA Ops:
  7.2 108.3 %copy-start = (bf16[768,768]{1,0:T(8,128)(2,1)S(1)}, bf16[768,768]{1,0:T(8,128)(2,1)}, u32[]{:S(2)}) copy-start(bf16[768,768]{1,0:T(8,128)(2,1)} %param.53) | copy-start | bytes 3538948
  7.2 3.8 copy-start.55
  7.2 3.8 copy-start.56
  7.2 222.3 %all-gather.27.cloned.1.call-start = ((), (), s32[]{:S(2)}) async-start(), calls=%async_computation.5 | async-start | bytes 2027520 | tf_op jit(solution)/shard_map/all_gather | solution.py:727
  105.3 10.2 %copy-start.57 = (bf16[768]{0:T(1024)(128)(2,1)S(1)}, bf16[768]{0:T(1024)(128)(2,1)}, u32[]{:S(2)}) copy-start(bf16[768]{0:T(1024)(128)(2,1)} %param.54) | copy-start | bytes 4612
  120.7 3.2 copy-start.47
  120.8 3.2 copy-start.58
  120.8 3.2 copy-start.59
  120.8 3.2 copy-start.60
  151.0 3.5 copy-start.61
  151.0 3.5 copy-start.62
  151.0 4.2 copy-start.3
  164.7 3.4 copy-start.29
  170.0 3.4 copy-start.71
  170.0 4.1 copy-start.15
  170.0 109.2 %all-gather.17.cloned.1.call-start = ((), (), s32[]{:S(2)}) async-start(), calls=%async_computation | async-start | bytes 5308416 | tf_op jit(solution)/shard_map/all_gather | solution.py:729
  170.8 151.3 %all-gather.19.cloned.1.call-start = ((), (), s32[]{:S(2)}) async-start(), calls=%async_computation.1 | async-start | bytes 1769472 | tf_op jit(solution)/shard_map/all_gather | solution.py:729
  171.5 3.3 copy-start.63
  171.5 8.9 %copy-start.64 = (bf16[384]{0:T(512)(128)(2,1)S(1)}, bf16[384]{0:T(512)(128)(2,1)}, u32[]{:S(2)}) copy-start(bf16[384]{0:T(512)(128)(2,1)} %param.37) | copy-start | bytes 2308
  171.5 13.3 %copy-start.65 = (bf16[384]{0:T(512)(128)(2,1)S(1)}, bf16[384]{0:T(512)(128)(2,1)}, u32[]{:S(2)}) copy-start(bf16[384]{0:T(512)(128)(2,1)} %param.40) | copy-start | bytes 2308
  171.5 18.3 %copy-start.50 = (bf16[1536]{0:T(1024)(128)(2,1)S(1)}, bf16[1536]{0:T(1024)(128)(2,1)}, u32[]{:S(2)}) copy-start(bf16[1536]{0:T(1024)(128)(2,1)} %param.44) | copy-start | bytes 9220
  171.5 23.3 %copy-start.66 = (bf16[384]{0:T(512)(128)(2,1)S(1)}, bf16[384]{0:T(512)(128)(2,1)}, u32[]{:S(2)}) copy-start(bf16[384]{0:T(512)(128)(2,1)} %param.41) | copy-start | bytes 2308
  171.6 28.2 %copy-start.67 = (bf16[384]{0:T(512)(128)(2,1)S(1)}, bf16[384]{0:T(512)(128)(2,1)}, u32[]{:S(2)}) copy-start(bf16[384]{0:T(512)(128)(2,1)} %param.42) | copy-start | bytes 2308
  171.6 33.1 %copy-start.68 = (bf16[384]{0:T(512)(128)(2,1)S(1)}, bf16[384]{0:T(512)(128)(2,1)}, u32[]{:S(2)}) copy-start(bf16[384]{0:T(512)(128)(2,1)} %param.46) | copy-start | bytes 2308
  171.6 38.1 %copy-start.69 = (bf16[384]{0:T(512)(128)(2,1)S(1)}, bf16[384]{0:T(512)(128)(2,1)}, u32[]{:S(2)}) copy-start(bf16[384]{0:T(512)(128)(2,1)} %param.47) | copy-start | bytes 2308
  171.6 42.4 %copy-start.70 = (bf16[384]{0:T(512)(128)(2,1)S(1)}, bf16[384]{0:T(512)(128)(2,1)}, u32[]{:S(2)}) copy-start(bf16[384]{0:T(512)(128)(2,1)} %param.48) | copy-start | bytes 2308
  171.6 196.1 %all-gather.21.cloned.1.call-start = ((), (), s32[]{:S(2)}) async-start(), calls=%async_computation.2 | async-start | bytes 7077888 | tf_op jit(solution)/shard_map/all_gather | solution.py:729
  172.2 259.6 %all-gather.23.cloned.1.call-start = ((), (), s32[]{:S(2)}) async-start(), calls=%async_computation.3 | async-start | bytes 7077888 | tf_op jit(solution)/shard_map/all_gather | solution.py:729
  172.8 283.2 %all-gather.25.cloned.1.call-start = ((), (), s32[]{:S(2)}) async-start(), calls=%async_computation.4 | async-start | bytes 1769472 | tf_op jit(solution)/shard_map/all_gather | solution.py:729
  174.7 15.1 %copy-start.36 = (f32[576]{0:T(1024)}, f32[576]{0:T(1024)S(1)}, u32[]{:S(2)}) copy-start(f32[576]{0:T(1024)S(1)} %fusion.67) | copy-start | bytes 6916
  174.8 110.4 %copy-start.34 = (f32[576]{0:T(1024)}, f32[576]{0:T(1024)S(1)}, u32[]{:S(2)}) copy-start(f32[576]{0:T(1024)S(1)} %fusion.93) | copy-start | bytes 6916
  180.4 104.7 %copy-start.32 = (f32[768]{0:T(1024)}, f32[768]{0:T(1024)S(1)}, u32[]{:S(2)}) copy-start(f32[768]{0:T(1024)S(1)} %reshape.397) | copy-start | bytes 9220
  184.8 100.3 %copy-start.39 = (f32[768]{0:T(1024)}, f32[768]{0:T(1024)S(1)}, u32[]{:S(2)}) copy-start(f32[768]{0:T(1024)S(1)} %reshape.398) | copy-start | bytes 9220
  299.1 15.9 %copy-start.25 = (bf16[36,16,1,12,64]{4,3,2,1,0:T(8,128)(2,1)}, bf16[36,16,1,12,64]{4,3,2,1,0:T(8,128)(2,1)S(1)}, u32[]{:S(2)}) copy-start(bf16[36,16,1,12,64]{4,3,2,1,0:T(8,128)(2,1)S(1)} %get-tuple-element.128) | copy-start | bytes 2654212
  317.5 4.6 copy-start.48
  322.0 45.7 %copy-start.41 = (f32[768]{0:T(1024)S(1)}, f32[768]{0:T(1024)}, u32[]{:S(2)}) copy-start(f32[768]{0:T(1024)} %reshape.400) | copy-start | bytes 9220
  322.1 45.7 %copy-start.42 = (f32[768]{0:T(1024)S(1)}, f32[768]{0:T(1024)}, u32[]{:S(2)}) copy-start(f32[768]{0:T(1024)} %reshape.401) | copy-start | bytes 9220
  322.1 45.7 %copy-start.45 = (f32[2,1,1536]{2,1,0:T(1,128)S(1)}, f32[2,1,1536]{2,1,0:T(1,128)}, u32[]{:S(2)}) copy-start(f32[2,1,1536]{2,1,0:T(1,128)} %convert_element_type.249) | copy-start | bytes 36868
  324.6 53.6 %copy-start.17 = (f32[576,768]{1,0:T(8,128)}, f32[576,768]{1,0:T(8,128)S(1)}, u32[]{:S(2)}) copy-start(f32[576,768]{1,0:T(8,128)S(1)} %get-tuple-element.136) | copy-start | bytes 5308420
  367.7 64.1 %copy-start.49 = (f32[768]{0:T(1024)S(1)}, f32[768]{0:T(1024)}, u32[]{:S(2)}) copy-start(f32[768]{0:T(1024)} %reshape.403) | copy-start | bytes 9220
  431.8 9.8 %copy-start.43 = (f32[768]{0:T(1024)S(1)}, f32[768]{0:T(1024)}, u32[]{:S(2)}) copy-start(f32[768]{0:T(1024)} %reshape.405) | copy-start | bytes 9220
  441.6 16.2 %copy-start.44 = (f32[36]{0:T(128)S(1)}, f32[36]{0:T(128)}, u32[]{:S(2)}) copy-start(f32[36]{0:T(128)} %get-tuple-element.118) | copy-start | bytes 436
  443.1 58.2 %copy-start.31 = (f32[36,768]{1,0:T(8,128)S(1)}, f32[36,768]{1,0:T(8,128)}, u32[]{:S(2)}) copy-start(f32[36,768]{1,0:T(8,128)} %copy-done.30) | copy-start | bytes 331780
  443.1 58.2 %copy-start.52 = (f32[36]{0:T(128)S(1)}, f32[36]{0:T(128)}, u32[]{:S(2)}) copy-start(f32[36]{0:T(128)} %copy-done.51) | copy-start | bytes 436
  457.7 2.8 copy-start.53
  507.3 3.4 copy-start.46
  509.0 12.3 %slice-start.2 = ((s8[4718592]{0:T(1024)(128)(4,1)}), s8[524288]{0:T(1024)(128)(4,1)S(1)}, s32[]{:S(2)}) async-start(s8[4718592]{0:T(1024)(128)(4,1)} %bitcast.146), calls=%async_computation.8 | async-start | bytes 1048576
  510.7 10.6 %copy-start.18 = (f32[576,768]{1,0:T(8,128)S(1)}, f32[576,768]{1,0:T(8,128)}, u32[]{:S(2)}) copy-start(f32[576,768]{1,0:T(8,128)} %copy-done.17) | copy-start | bytes 5308420
  510.7 10.6 %slice-start.3 = ((s8[4718592]{0:T(1024)(128)(4,1)}), s8[4194304]{0:T(1024)(128)(4,1)S(1)}, s32[]{:S(2)}) async-start(s8[4718592]{0:T(1024)(128)(4,1)} %bitcast.146), calls=%async_computation.9 | async-start | bytes 8388608
  521.3 3.4 copy-start.24
  534.0 5.2 copy-start.14
  534.0 5.2 copy-start.28
  542.6 4.9 copy-start.7
  553.5 9.5 %copy-start.33 = (f32[768]{0:T(1024)S(1)}, f32[768]{0:T(1024)}, u32[]{:S(2)}) copy-start(f32[768]{0:T(1024)} %copy-done.32) | copy-start | bytes 9220
  562.9 5.2 copy-start.37
  562.9 6.4 copy-start.35
  571.4 4.1 copy-start.5
  571.4 5.2 copy-start.8
  597.9 4.5 copy-start.20
  597.9 4.5 copy-start.40
  623.2 5.4 copy-start.23
  762.3 12.3 %slice-start = ((s8[7667712]{0:T(1024)(128)(4,1)}), s8[3473408]{0:T(1024)(128)(4,1)S(1)}, s32[]{:S(2)}) async-start(s8[7667712]{0:T(1024)(128)(4,1)} %bitcast.129), calls=%async_computation.6 | async-start | bytes 6946816
  767.3 7.4 slice-start.1
  797.5 49.3 %copy-start.1 = (bf16[768,768]{1,0:T(8,128)(2,1)S(1)}, bf16[768,768]{1,0:T(8,128)(2,1)}, u32[]{:S(2)}) copy-start(bf16[768,768]{1,0:T(8,128)(2,1)} %param.53) | copy-start | bytes 3538948
  (19 other events, 32.9 us)
Sparse Core Ops, SparseCore 0:
  170.1 59.3 all-gather.26
  231.0 48.1 all-gather.16
  280.8 22.7 all-gather.18
  305.0 62.6 all-gather.20
  369.1 62.6 all-gather.22
  433.2 22.7 all-gather.24

commit v2 on v1

--- a/solution.py
+++ b/solution.py
@@ -1,5 +1,3 @@
-import functools
-
 import jax
 import jax.numpy as jnp
 from jax import lax
@@ -235,6 +233,832 @@
 MESH = pl.DeviceIdType.MESH
 
 
+ROOT_SCALE = 0.125
+PAIR = 128
+CUT = -1e30
+TEXT_GROUP = 96
+CHUNK = 96
+SLOT_ROWS = 40
+NEAR = 8
+GELU_ROOT = 0.7978845608028654
+GELU_CUBE = 0.044715
+
+
+def wide(values):
+    return values.astype(jnp.float32)
+
+
+def low(values):
+    return values.astype(jnp.bfloat16)
+
+
+def centred_scale(values):
+    centred = values - jnp.mean(values, axis=-1, keepdims=True)
+    variance = jnp.mean(centred * centred, axis=-1, keepdims=True)
+    rate = lax.rsqrt(variance + EPSILON)
+    return centred * rate, rate
+
+
+def gelu_value(values):
+    inner = GELU_ROOT * (values + GELU_CUBE * (values * values * values))
+    half = 0.5 * values
+    return half + half * jnp.tanh(inner)
+
+
+def gelu_slope(values):
+    square = values * values
+    bend = jnp.tanh(GELU_ROOT * values * (1.0 + GELU_CUBE * square))
+    inner_slope = GELU_ROOT * (1.0 + (3.0 * GELU_CUBE) * square)
+    return 0.5 * (1.0 + bend) + 0.5 * values * (1.0 - bend * bend) * inner_slope
+
+
+def norm_back(values, grad, gain):
+    unit, rate = centred_scale(values)
+    scaled = grad * gain
+    mean = jnp.mean(scaled, axis=-1, keepdims=True)
+    slope = jnp.mean(scaled * unit, axis=-1, keepdims=True)
+    return rate * (scaled - mean - unit * slope), grad * unit
+
+
+def column_sum(values):
+    return jnp.sum(values, axis=0, keepdims=True)
+
+
+def peers_of(dp, x):
+    z, y, core = dp // 4, (dp // 2) % 2, dp % 2
+    near = []
+    for step in range(1, NEAR):
+        flip_x, flip_y, flip_core = step % 2, (step // 2) % 2, step // 4
+        other_y = y + flip_y - 2 * flip_y * y
+        other_core = core + flip_core - 2 * flip_core * core
+        other_x = x + flip_x - 2 * flip_x * x
+        near.append((z * 4 + other_y * 2 + other_core, other_x))
+    far = [(((z + step) % 4) * 4 + y * 2 + core, x) for step in range(1, 4)]
+    return near, far
+
+
+def text_body(
+    token_ref,
+    vector_ref,
+    image_ref,
+    live_ref,
+    own_live_ref,
+    scale_ref,
+    joint_hbm,
+    mixer_hbm,
+    up_hbm,
+    down_hbm,
+    project_hbm,
+    left_hbm,
+    right_hbm,
+    vector_out,
+    token_out,
+    joint,
+    mixer,
+    up,
+    down,
+    project,
+    left,
+    right,
+    triple,
+    residual,
+    active_in,
+    output,
+    work,
+    images,
+    near_sums,
+    far_sums,
+    weight_sem,
+    image_sem,
+    near_sem,
+    far_sem,
+    store_sem,
+):
+    dp = lax.axis_index("dp")
+    x = lax.axis_index("fsdp")
+    z, y, core = dp // 4, (dp // 2) % 2, dp % 2
+    near, far = peers_of(dp, x)
+    x_peer, y_peer, core_peer = near[0], near[1], near[3]
+    loads = [
+        pltpu.make_async_copy(source, target, weight_sem.at[index])
+        for index, (source, target) in enumerate(
+            (
+                (joint_hbm, joint),
+                (mixer_hbm, mixer),
+                (up_hbm, up),
+                (down_hbm, down),
+                (project_hbm, project),
+            )
+        )
+    ]
+    for load in loads:
+        load.start()
+    barrier = pltpu.get_barrier_semaphore()
+    for peer in near + far:
+        pl.semaphore_signal(barrier, inc=1, device_id=peer, device_id_type=MESH)
+
+    def send(source, target, sems, index, peer):
+        return pltpu.make_async_remote_copy(
+            src_ref=source,
+            dst_ref=target,
+            send_sem=sems.at[0, index],
+            recv_sem=sems.at[1, index],
+            device_id=peer,
+            device_id_type=MESH,
+        )
+
+    own_slot = images.at[core, y, x, z]
+    z_sends = [send(own_slot, own_slot, image_sem, k, far[k]) for k in range(3)]
+    line = images.at[core, y, x]
+    y_send = send(line, line, image_sem, 3, y_peer)
+    x_send = send(line, line, image_sem, 4, x_peer)
+    other_line = images.at[core, 1 - y, x]
+    x_again = send(other_line, other_line, image_sem, 5, x_peer)
+    plane = images.at[core]
+    core_send = send(plane, plane, image_sem, 6, core_peer)
+
+    rows, width = token_ref.shape
+    feed = up.shape[1]
+    seqs = rows // TEXT_LEN
+
+    def vector(index):
+        return wide(jnp.concatenate([vector_ref[0, index], vector_ref[1, index]], axis=1))
+
+    def span(index, size):
+        return pl.ds(pl.multiple_of(index * size, size), size)
+
+    gain, offset, mix_bias, feed_gain, feed_offset, down_bias, end_gain, end_offset = (
+        vector(index) for index in range(8)
+    )
+    images[core, y, x, z] = image_ref[...]
+
+    @pl.loop(0, rows // CHUNK)
+    def _(index):
+        chunk = span(index, CHUNK)
+        unit, rate = centred_scale(wide(token_ref[chunk]))
+        left[6, chunk] = low(unit * gain + offset)
+
+    loads[0].wait()
+    pl.semaphore_wait(barrier, 10)
+    for copy in z_sends:
+        copy.start()
+
+    @pl.loop(0, 3)
+    def _(index):
+        cols = span(index, width)
+        triple[:, cols] = low(product(left[6], joint[:, cols]))
+
+    for copy in z_sends:
+        copy.wait()
+    x_send.start()
+    y_send.start()
+
+    lane = lax.broadcasted_iota(jnp.int32, (TEXT_GROUP, PAIR), 1) < HEAD_DIM
+    row_seq = lax.broadcasted_iota(jnp.int32, (2 * TEXT_GROUP, TEXT_GROUP), 0)
+    row_seq = jnp.where(row_seq >= TEXT_GROUP, row_seq - TEXT_GROUP, row_seq) // TEXT_LEN
+    col_seq = lax.broadcasted_iota(jnp.int32, (2 * TEXT_GROUP, TEXT_GROUP), 1) // TEXT_LEN
+    same = jnp.where(row_seq == col_seq, 0.0, CUT)
+    pairs = width // PAIR
+
+    def split_heads(values):
+        return low(
+            jnp.concatenate([jnp.where(lane, values, 0.0), jnp.where(lane, 0.0, values)], axis=0)
+        )
+
+    def join_heads(values):
+        return jnp.where(lane, values[:TEXT_GROUP], values[TEXT_GROUP:])
+
+    def head_scores(group, pair):
+        query = split_heads(wide(triple[group, pl.ds(pair * PAIR, PAIR)]) * ROOT_SCALE)
+        keys = triple[group, pl.ds(width + pair * PAIR, PAIR)]
+        values = triple[group, pl.ds(2 * width + pair * PAIR, PAIR)]
+        scores = contract_last(query, keys) + same
+        return query, keys, values, jnp.exp(scores - jnp.max(scores, axis=-1, keepdims=True))
+
+    @pl.loop(0, rows // TEXT_GROUP)
+    def _(index):
+        group = span(index, TEXT_GROUP)
+        for pair in range(pairs):
+            query, keys, values, soft = head_scores(group, pair)
+            mixed = product(low(soft), jnp.concatenate([values, jnp.ones_like(values)], axis=1))
+            mixed = mixed[:, :PAIR] / mixed[:, PAIR:]
+            left[5, group, pl.ds(pair * PAIR, PAIR)] = low(join_heads(mixed))
+
+    x_send.wait()
+    y_send.wait()
+    x_again.start()
+    loads[1].wait()
+    residual[...] = product(left[5], mixer[...])
+
+    @pl.loop(0, rows // CHUNK)
+    def _(index):
+        chunk = span(index, CHUNK)
+        values = wide(token_ref[chunk]) + residual[chunk] + mix_bias
+        residual[chunk] = values
+        unit, rate = centred_scale(values)
+        left[4, chunk] = low(unit * feed_gain + feed_offset)
+
+    loads[2].wait()
+    for index in range(feed // width):
+        cols = pl.ds(index * width, width)
+        bias = jnp.concatenate(
+            [vector_ref[index // 2, 8 + (index % 2) * 2 + part] for part in range(2)], axis=1
+        )
+        values = product(left[4], up[:, cols]) + wide(bias)
+        active_in[:, cols] = values
+        values = low(gelu_value(values))
+        for part in range(2):
+            block = index * 2 + part
+            left[block % 4, :, pl.ds((block // 4) * HALF, HALF)] = values[
+                :, part * HALF : (part + 1) * HALF
+            ]
+    x_again.wait()
+    core_send.start()
+    loads[3].wait()
+    total = None
+    for block in range(4):
+        for side in range(2):
+            term = product(
+                left[block, :, pl.ds(side * HALF, HALF)],
+                down[pl.ds(side * 2 * width + block * HALF, HALF)],
+            )
+            total = term if total is None else total + term
+    output[...] = total
+
+    @pl.loop(0, rows // CHUNK)
+    def _(index):
+        chunk = span(index, CHUNK)
+        values = residual[chunk] + output[chunk] + down_bias
+        output[chunk] = values
+        unit, rate = centred_scale(values)
+        work[span(index, 8), :] = jnp.pad(
+            jnp.sum(unit.reshape(CHUNK // TEXT_LEN, TEXT_LEN, width), axis=1), ((0, 2), (0, 0))
+        )
+
+    pooled = jnp.concatenate(
+        [work[index * 8 : index * 8 + CHUNK // TEXT_LEN] for index in range(rows // CHUNK)], axis=0
+    )
+    pooled = low(pooled * (1.0 / TEXT_LEN) * end_gain + end_offset)
+    loads[4].wait()
+    embedding = product(pooled, project[...])
+    length_rate = lax.rsqrt(jnp.sum(embedding * embedding, axis=-1, keepdims=True) + EPSILON)
+    text_unit = embedding * length_rate
+    text_low = low(text_unit)
+    core_send.wait()
+
+    every = images[...].reshape(2 * 2 * 2 * 4 * SLOT_ROWS, width)
+    live = live_ref[...]
+    own_live = own_live_ref[...]
+    temper = jnp.exp(scale_ref[...])
+    live_total = jnp.sum(live, axis=1, keepdims=True)
+    half_inverse = 0.5 / live_total
+    cosine = contract_last(text_low, every)
+    scaled = jnp.exp(temper * cosine - temper)
+    row_sum = jnp.sum(scaled * live, axis=1, keepdims=True)
+    near_place = x + 2 * y + 4 * core
+    near_sums[near_place] = column_sum(scaled * own_live)
+    near_sends = [
+        send(near_sums.at[near_place], near_sums.at[near_place], near_sem, k, near[k])
+        for k in range(NEAR - 1)
+    ]
+    for copy in near_sends:
+        copy.start()
+    image_own = wide(image_ref[:seqs])
+    diagonal_cos = jnp.sum(wide(text_low) * image_own, axis=1, keepdims=True)
+    row_part = scaled * (own_live / row_sum) * live
+    for copy in near_sends:
+        copy.wait()
+    far_sums[z] = (
+        ((near_sums[0] + near_sums[1]) + (near_sums[2] + near_sums[3]))
+        + ((near_sums[4] + near_sums[5]) + (near_sums[6] + near_sums[7]))
+    )
+    far_sends = [
+        send(far_sums.at[z], far_sums.at[z], far_sem, k, far[k]) for k in range(3)
+    ]
+    for copy in far_sends:
+        copy.start()
+    for copy in far_sends:
+        copy.wait()
+    columns = (far_sums[0] + far_sums[1]) + (far_sums[2] + far_sums[3])
+    coupling = (row_part + scaled * own_live * (live / columns)) * half_inverse
+    column_log = jnp.where(live > 0.0, temper + jnp.log(columns), 0.0)
+    row_log = temper + jnp.log(row_sum)
+    loss_own = column_sum(own_live * (row_log - 2.0 * temper * diagonal_cos))
+    loss_shared = jnp.sum(live * column_log, axis=1, keepdims=True)
+    devices = lax.axis_size("dp") * lax.axis_size("fsdp")
+    loss_part = (loss_own + loss_shared * (1.0 / devices)) * half_inverse
+    temper_grad = (
+        jnp.sum(column_sum(coupling * cosine), axis=1, keepdims=True)
+        - column_sum(own_live * diagonal_cos) / live_total
+    )
+    unit_grad = product(low(temper * coupling), every)
+    unit_grad = unit_grad - (temper / live_total) * own_live * image_own
+    embed_grad = low(
+        (unit_grad - text_unit * jnp.sum(text_unit * unit_grad, axis=-1, keepdims=True))
+        * length_rate
+    )
+    left[7] = jnp.zeros((rows, width), jnp.bfloat16)
+    left[7, :SLOT_ROWS] = jnp.pad(pooled, ((0, SLOT_ROWS - seqs), (0, 0)))
+    right[9] = jnp.zeros((rows, width), jnp.bfloat16)
+    right[9, :SLOT_ROWS] = jnp.pad(embed_grad, ((0, SLOT_ROWS - seqs), (0, 0)))
+    pooled_grad = contract_last(embed_grad, project[...]) * (1.0 / TEXT_LEN)
+    for index in range(rows // CHUNK):
+        work[index * 8 : index * 8 + CHUNK // TEXT_LEN] = pooled_grad[
+            index * (CHUNK // TEXT_LEN) : (index + 1) * (CHUNK // TEXT_LEN)
+        ]
+
+    vector_out[...] = jnp.zeros(vector_out.shape, jnp.float32)
+    column = lax.broadcasted_iota(jnp.int32, (1, width), 1)
+    vector_out[12:13] = jnp.where(
+        column == 0, loss_part, jnp.where(column == 1, temper * temper_grad, 0.0)
+    )
+    vector_out[11:12] = column_sum(pooled_grad) * float(TEXT_LEN)
+
+    def gather(index, value):
+        vector_out[index : index + 1] = vector_out[index : index + 1] + value
+
+    @pl.loop(0, rows // CHUNK)
+    def _(index):
+        chunk = span(index, CHUNK)
+        grad = work[span(index, 8)][: CHUNK // TEXT_LEN]
+        grad = jnp.broadcast_to(
+            grad[:, None, :], (CHUNK // TEXT_LEN, TEXT_LEN, width)
+        ).reshape(CHUNK, width)
+        value, gain_part = norm_back(output[chunk], grad, end_gain)
+        output[chunk] = value
+        right[0, chunk] = low(value)
+        gather(10, column_sum(gain_part))
+        gather(9, column_sum(value))
+
+    stores = []
+
+    def store(source, target):
+        copy = pltpu.make_async_copy(source, target, store_sem.at[len(stores)])
+        copy.start()
+        stores.append(copy)
+
+    for slab in (0, 1, 2, 3, 4, 5, 6, 7):
+        store(left.at[slab], left_hbm.at[slab])
+    for slab in (0, 9):
+        store(right.at[slab], right_hbm.at[slab])
+
+    for index in range(feed // width):
+        cols = pl.ds(index * width, width)
+        values = contract_last(right[0], down[cols]) * gelu_slope(active_in[:, cols])
+        vector_out[5 + index : 6 + index] = column_sum(values)
+        right[1 + index] = low(values)
+        store(right.at[1 + index], right_hbm.at[1 + index])
+
+    total = None
+    for index in range(feed // width):
+        term = contract_last(right[1 + index], up[:, pl.ds(index * width, width)])
+        total = term if total is None else total + term
+    active_in[:, :width] = total
+
+    @pl.loop(0, rows // CHUNK)
+    def _(index):
+        chunk = span(index, CHUNK)
+        grad = active_in[chunk, :width]
+        value, gain_part = norm_back(residual[chunk], grad, feed_gain)
+        value = value + output[chunk]
+        output[chunk] = value
+        right[5, chunk] = low(value)
+        gather(3, column_sum(gain_part))
+        gather(4, column_sum(grad))
+        gather(2, column_sum(value))
+
+    store(right.at[5], right_hbm.at[5])
+    active_in[:, width : 2 * width] = contract_last(right[5], mixer[...])
+
+    @pl.loop(0, rows // TEXT_GROUP)
+    def _(index):
+        group = span(index, TEXT_GROUP)
+        for pair in range(pairs):
+            cols = pl.ds(pair * PAIR, PAIR)
+            query, keys, values, soft = head_scores(group, pair)
+            soft = soft / jnp.sum(soft, axis=-1, keepdims=True)
+            outer = split_heads(active_in[group, pl.ds(width + pair * PAIR, PAIR)])
+            soft_grad = contract_last(outer, values)
+            score_grad = low(
+                soft * (soft_grad - jnp.sum(soft * soft_grad, axis=-1, keepdims=True))
+            )
+            right[6, group, cols] = low(join_heads(product(score_grad, keys)) * ROOT_SCALE)
+            right[7, group, cols] = low(contract_first(score_grad, query))
+            right[8, group, cols] = low(contract_first(low(soft), outer))
+
+    for index in range(3):
+        store(right.at[6 + index], right_hbm.at[6 + index])
+    total = None
+    for index in range(3):
+        term = contract_last(right[6 + index], joint[:, pl.ds(index * width, width)])
+        total = term if total is None else total + term
+    active_in[:, :width] = total
+
+    @pl.loop(0, rows // CHUNK)
+    def _(index):
+        chunk = span(index, CHUNK)
+        grad = active_in[chunk, :width]
+        value, gain_part = norm_back(wide(token_ref[chunk]), grad, gain)
+        token_out[chunk] = value + output[chunk]
+        gather(0, column_sum(gain_part))
+        gather(1, column_sum(grad))
+
+    for copy in stores:
+        copy.wait()
+
+
+def text_kernel(tokens, vectors, image_low, live, own_live, log_scale, weights):
+    rows, width = tokens.shape
+    joint, mixer, up, down, project = weights
+    any_spec = pl.BlockSpec(memory_space=pl.ANY)
+    vmem_spec = pl.BlockSpec(memory_space=pltpu.VMEM)
+    dma = pltpu.SemaphoreType.DMA
+    low_type = jnp.bfloat16
+    padded = jnp.pad(image_low, ((0, SLOT_ROWS - image_low.shape[0]), (0, 0)))
+    slots = 2 * 2 * 2 * 4 * SLOT_ROWS
+    return pl.pallas_call(
+        text_body,
+        out_shape=(
+            jax.ShapeDtypeStruct((FACTOR_A, rows, width), low_type),
+            jax.ShapeDtypeStruct((FACTOR_B, rows, width), low_type),
+            jax.ShapeDtypeStruct((VECTOR_ROWS, width), jnp.float32),
+            jax.ShapeDtypeStruct((rows, width), jnp.float32),
+        ),
+        in_specs=[vmem_spec] * 6 + [any_spec] * 5,
+        out_specs=(any_spec, any_spec, vmem_spec, vmem_spec),
+        scratch_shapes=[pltpu.VMEM(weight.shape, low_type) for weight in weights]
+        + [
+            pltpu.VMEM((FACTOR_A, rows, width), low_type),
+            pltpu.VMEM((FACTOR_B, rows, width), low_type),
+            pltpu.VMEM((rows, 3 * width), low_type),
+            pltpu.VMEM((rows, width), jnp.float32),
+            pltpu.VMEM((rows, up.shape[1]), jnp.float32),
+            pltpu.VMEM((rows, width), jnp.float32),
+            pltpu.VMEM((rows // CHUNK * 8, width), jnp.float32),
+            pltpu.VMEM((2, 2, 2, 4, SLOT_ROWS, width), low_type),
+            pltpu.VMEM((NEAR, 1, slots), jnp.float32),
+            pltpu.VMEM((4, 1, slots), jnp.float32),
+            dma((5,)),
+            dma((2, 7)),
+            dma((2, NEAR - 1)),
+            dma((2, 3)),
+            dma((FACTOR_A + FACTOR_B,)),
+        ],
+        compiler_params=pltpu.CompilerParams(
+            collective_id=1, has_side_effects=True, vmem_limit_bytes=62 * 1024 * 1024
+        ),
+    )(tokens, vectors, padded, live, own_live, log_scale.reshape(1, 1), *weights)
+
+
+IMAGE_GROUP = 4
+IMAGE_BLOCK = 12
+IMAGE_CHUNK = 120
+IMAGE_ROWS = 104
+IMAGE_KEYS = 128
+
+
+def image_body(
+    token_ref,
+    vector_ref,
+    bias_ref,
+    shard_vector,
+    joint_hbm,
+    mixer_hbm,
+    up_hbm,
+    down_hbm,
+    project_hbm,
+    joint_shard,
+    mixer_shard,
+    up_shard,
+    down_shard,
+    project_shard,
+    image_out,
+    vector_out,
+    joint_full,
+    mixer_full,
+    up_full,
+    down_full,
+    project_full,
+    joint,
+    mixer,
+    up,
+    down,
+    project,
+    normed,
+    triple,
+    attended,
+    residual,
+    hidden,
+    pooled,
+    load_sem,
+    own_sem,
+    x_sem,
+    y_sem,
+    core_sem,
+):
+    dp = lax.axis_index("dp")
+    x = lax.axis_index("fsdp")
+    y, core = (dp // 2) % 2, dp % 2
+    x_peer, y_peer, core_peer = (dp, 1 - x), (dp + 2 - 4 * y, x), (dp + 1 - 2 * core, x)
+    loads = [
+        pltpu.make_async_copy(source, target, load_sem.at[index])
+        for index, (source, target) in enumerate(
+            (
+                (joint_hbm, joint),
+                (mixer_hbm, mixer),
+                (up_hbm, up),
+                (down_hbm, down),
+                (project_hbm, project),
+            )
+        )
+    ]
+    for load in loads:
+        load.start()
+    barrier = pltpu.get_barrier_semaphore()
+    for peer in (x_peer, y_peer, core_peer):
+        pl.semaphore_signal(barrier, inc=1, device_id=peer, device_id_type=MESH)
+    vector_out[x] = shard_vector[...]
+    pl.semaphore_wait(barrier, 3)
+
+    def send(source, target, sems, index, peer):
+        return pltpu.make_async_remote_copy(
+            src_ref=source,
+            dst_ref=target,
+            send_sem=sems.at[0, index],
+            recv_sem=sems.at[1, index],
+            device_id=peer,
+            device_id_type=MESH,
+        )
+
+    shards = (joint_shard, mixer_shard, up_shard, down_shard, project_shard)
+    fulls = (joint_full, mixer_full, up_full, down_full, project_full)
+    own_copies, x_sends, y_sends, core_sends = [], [], [], []
+    for index, (shard, full) in enumerate(zip(shards, fulls)):
+        half = shard.shape[0]
+        quarter = half // 4
+        piece = core * 2 + y
+
+        def rows(start, size):
+            return pl.ds(pl.multiple_of(start, quarter), size)
+
+        own_copies.append(
+            pltpu.make_async_copy(shard, full.at[rows(x * half, half)], own_sem.at[index])
+        )
+        x_sends.append(
+            send(
+                shard.at[rows(piece * quarter, quarter)],
+                full.at[rows(x * half + piece * quarter, quarter)],
+                x_sem,
+                index,
+                x_peer,
+            )
+        )
+        got = full.at[rows((1 - x) * half + piece * quarter, quarter)]
+        y_sends.append(send(got, got, y_sem, index, y_peer))
+        pair = full.at[rows((1 - x) * half + core * 2 * quarter, 2 * quarter)]
+        core_sends.append(send(pair, pair, core_sem, index, core_peer))
+    x_sends.append(send(vector_out.at[x], vector_out.at[x], x_sem, 5, x_peer))
+    for copy in x_sends:
+        copy.start()
+    for copy in own_copies:
+        copy.start()
+
+    def pass_y(index):
+        x_sends[index].wait()
+        y_sends[index].start()
+
+    def pass_core(index):
+        y_sends[index].wait()
+        core_sends[index].start()
+
+    blocks, rows, width = token_ref.shape
+    feed = up.shape[1]
+    gain, offset, mix_bias, feed_gain, feed_offset, down_bias, end_gain, end_offset = (
+        wide(vector_ref[index : index + 1]) for index in range(8)
+    )
+
+    def span(index, size):
+        return pl.ds(pl.multiple_of(index * size, 8), size)
+
+    seqs = rows // IMAGE_LEN
+    pool_row = lax.broadcasted_iota(jnp.int32, (seqs, rows), 0)
+    pool_col = lax.broadcasted_iota(jnp.int32, (seqs, rows), 1) // IMAGE_LEN
+    pool = low(jnp.where(pool_row == pool_col, 1.0, 0.0))
+    group_rows = IMAGE_GROUP * IMAGE_LEN
+    lane = lax.broadcasted_iota(jnp.int32, (IMAGE_ROWS, PAIR), 1) < HEAD_DIM
+    seam = lax.broadcasted_iota(jnp.int32, (8, PAIR), 0) < 4
+    windows = []
+    for row_start, key_start in (
+        (0, 0),
+        (group_rows - IMAGE_ROWS, group_rows - IMAGE_KEYS),
+    ):
+        row = lax.broadcasted_iota(jnp.int32, (2 * IMAGE_ROWS, IMAGE_KEYS), 0)
+        row = jnp.where(row >= IMAGE_ROWS, row - IMAGE_ROWS, row) + row_start
+        col = lax.broadcasted_iota(jnp.int32, (2 * IMAGE_ROWS, IMAGE_KEYS), 1) + key_start
+        same = jnp.where(row // IMAGE_LEN == col // IMAGE_LEN, 0.0, CUT)
+        windows.append((row_start, key_start, same))
+
+    def attend(start, pair):
+        cols = pair * PAIR
+        parts = []
+        for row_start, key_start, same in windows:
+            query = (
+                wide(triple[pl.ds(start + row_start, IMAGE_ROWS), pl.ds(cols, PAIR)]) * ROOT_SCALE
+            )
+            keys = triple[pl.ds(start + key_start, IMAGE_KEYS), pl.ds(width + cols, PAIR)]
+            values = triple[pl.ds(start + key_start, IMAGE_KEYS), pl.ds(2 * width + cols, PAIR)]
+            heads = low(
+                jnp.concatenate([jnp.where(lane, query, 0.0), jnp.where(lane, 0.0, query)], axis=0)
+            )
+            scores = contract_last(heads, keys) + same
+            soft = low(jnp.exp(scores - jnp.max(scores, axis=-1, keepdims=True)))
+            mixed = product(soft, jnp.concatenate([values, jnp.ones_like(values)], axis=1))
+            mixed = mixed[:, :PAIR] / mixed[:, PAIR:]
+            parts.append(jnp.where(lane, mixed[:IMAGE_ROWS], mixed[IMAGE_ROWS:]))
+        first, second = parts
+        edge = IMAGE_ROWS - 8
+        attended[pl.ds(start, edge), pl.ds(cols, PAIR)] = low(first[:edge])
+        attended[pl.ds(start + edge, 8), pl.ds(cols, PAIR)] = low(
+            jnp.where(seam, first[edge:], second[:8])
+        )
+        attended[pl.ds(start + IMAGE_ROWS, edge), pl.ds(cols, PAIR)] = low(second[8:])
+
+    @pl.loop(0, blocks)
+    def _(block):
+        @pl.loop(0, rows // IMAGE_CHUNK)
+        def _(index):
+            chunk = span(index, IMAGE_CHUNK)
+            normed[chunk] = low(
+                centred_scale(wide(token_ref[block, chunk]))[0] * gain + offset
+            )
+
+        @pl.when(block == 0)
+        def _():
+            loads[0].wait()
+
+        @pl.when(block == 1)
+        def _():
+            pass_y(1)
+
+        @pl.when(block == 2)
+        def _():
+            pass_y(3)
+
+        for index in range(3):
+            cols = pl.ds(index * width, width)
+            triple[:, cols] = low(product(normed[...], joint[:, cols]))
+
+        @pl.loop(0, rows // group_rows)
+        def _(group):
+            start = pl.multiple_of(group * group_rows, 8)
+            for pair in range(width // PAIR):
+                attend(start, pair)
+
+        @pl.when(block == 0)
+        def _():
+            loads[1].wait()
+
+        @pl.when(block == 1)
+        def _():
+            pass_y(2)
+            pass_core(0)
+
+        @pl.when(block == 2)
+        def _():
+            pass_y(4)
+            pass_core(1)
+            pass_core(2)
+
+        residual[...] = product(attended[...], mixer[...])
+
+        @pl.loop(0, rows // IMAGE_CHUNK)
+        def _(index):
+            chunk = span(index, IMAGE_CHUNK)
+            values = wide(token_ref[block, chunk]) + residual[chunk] + mix_bias
+            residual[chunk] = values
+            normed[chunk] = low(centred_scale(values)[0] * feed_gain + feed_offset)
+
+        @pl.when(block == 0)
+        def _():
+            loads[2].wait()
+
+        for index in range(feed // width):
+            cols = pl.ds(index * width, width)
+            hidden[:, cols] = low(
+                gelu_value(product(normed[...], up[:, cols]) + wide(bias_ref[:, cols]))
+            )
+
+        @pl.when(block == 0)
+        def _():
+            loads[3].wait()
+            pass_y(0)
+
+        @pl.when(block == 2)
+        def _():
+            pass_core(3)
+
+        normed_sum = product(hidden[...], down[...])
+        residual[...] = residual[...] + normed_sum
+
+        @pl.loop(0, rows // IMAGE_CHUNK)
+        def _(index):
+            chunk = span(index, IMAGE_CHUNK)
+            normed[chunk] = low(centred_scale(residual[chunk] + down_bias)[0])
+
+        mean = product(pool, normed[...]) * (1.0 / IMAGE_LEN)
+        pooled[block] = mean * end_gain + end_offset
+
+    pass_core(4)
+    loads[4].wait()
+    for block in range(blocks):
+        embedding = product(low(pooled[block]), project[...])
+        image_out[block] = low(
+            embedding
+            * lax.rsqrt(jnp.sum(embedding * embedding, axis=-1, keepdims=True) + EPSILON)
+        )
+    for copy in core_sends + own_copies:
+        copy.wait()
+    x_sends[5].wait()
+
+
+def image_kernel(tokens, weights, shard_vector, shards):
+    (
+        norm_gain,
+        norm_offset,
+        joint,
+        mixer,
+        mixer_bias,
+        feed_gain,
+        feed_offset,
+        up,
+        up_bias,
+        down,
+        down_bias,
+        end_gain,
+        end_offset,
+        project,
+    ) = weights
+    total, width = tokens.shape
+    rows = IMAGE_BLOCK * IMAGE_LEN
+    blocks = total // rows
+    feed = up.shape[1]
+    vectors = jnp.stack(
+        [
+            norm_gain,
+            norm_offset,
+            mixer_bias,
+            feed_gain,
+            feed_offset,
+            down_bias,
+            end_gain,
+            end_offset,
+        ]
+    )
+    any_spec = pl.BlockSpec(memory_space=pl.ANY)
+    vmem_spec = pl.BlockSpec(memory_space=pltpu.VMEM)
+    dma = pltpu.SemaphoreType.DMA
+    low_type = jnp.bfloat16
+    matrices = (joint, mixer, up, down, project)
+    image_out, vector_out, *fulls = pl.pallas_call(
+        image_body,
+        out_shape=(
+            jax.ShapeDtypeStruct((blocks, IMAGE_BLOCK, width), low_type),
+            jax.ShapeDtypeStruct((2, *shard_vector.shape), low_type),
+            *(
+                jax.ShapeDtypeStruct((2 * shard.shape[0], shard.shape[1]), low_type)
+                for shard in shards
+            ),
+        ),
+        in_specs=[vmem_spec] * 4 + [any_spec] * 10,
+        out_specs=(vmem_spec, vmem_spec, *([any_spec] * 5)),
+        scratch_shapes=[pltpu.VMEM(matrix.shape, low_type) for matrix in matrices]
+        + [
+            pltpu.VMEM((rows, width), low_type),
+            pltpu.VMEM((rows, 3 * width), low_type),
+            pltpu.VMEM((rows, width), low_type),
+            pltpu.VMEM((rows, width), jnp.float32),
+            pltpu.VMEM((rows, feed), low_type),
+            pltpu.VMEM((blocks, IMAGE_BLOCK, width), jnp.float32),
+            dma((5,)),
+            dma((5,)),
+            dma((2, 6)),
+            dma((2, 5)),
+            dma((2, 5)),
+        ],
+        compiler_params=pltpu.CompilerParams(
+            collective_id=2, has_side_effects=True, vmem_limit_bytes=60 * 1024 * 1024
+        ),
+    )(
+        tokens.reshape(blocks, rows, width),
+        vectors,
+        up_bias.reshape(1, feed),
+        shard_vector,
+        *matrices,
+        *shards,
+    )
+    return image_out.reshape(total // IMAGE_LEN, width), vector_out, fulls
+
+
 def factor_a(unit):
     return jnp.minimum(unit, 4) + jnp.clip(unit - 7, 0, 2) + jnp.maximum(unit - 11, 0)
 
@@ -249,6 +1073,7 @@
     vector_ref,
     grad_hbm,
     vector_out,
+    a_raw,
     a_vmem,
     b_vmem,
     core_out,
@@ -291,13 +1116,9 @@
     pair_peer = (z_pair * 4 + y * 2 + core, x)
     mid_peer = ((3 - z) * 4 + y * 2 + core, x)
 
-    a_copies = [pltpu.make_async_copy(a_hbm.at[k], a_vmem.at[k], a_sem.at[k]) for k in range(FACTOR_A)]
-    b_copies = [pltpu.make_async_copy(b_hbm.at[k], b_vmem.at[k], b_sem.at[k]) for k in range(FACTOR_B)]
-    for unit in range(UNITS):
-        if unit < 5 or unit in (8, 9, 12):
-            a_copies[min(unit, 4) + min(max(unit - 7, 0), 2) + max(unit - 11, 0)].start()
-        if unit == 0 or unit >= 4:
-            b_copies[max(unit - 3, 0)].start()
+    pltpu.make_async_copy(a_hbm.at[0], a_raw, a_sem).start()
+    for slot in range(FACTOR_B):
+        pltpu.make_async_copy(b_hbm.at[slot], b_vmem.at[slot], b_sem.at[slot]).start()
 
     barrier = pltpu.get_barrier_semaphore()
     for peer in (core_peer, x_peer, y_peer):
@@ -368,12 +1189,6 @@
             remote(vector_sum.at[2], vector_z.at[step - 1], vector_sems, 2 + step, (other, x))
         )
 
-    def wide(values):
-        return values.astype(jnp.float32)
-
-    def low(values):
-        return values.astype(jnp.bfloat16)
-
     @pl.loop(0, STEPS + 8)
     def _(time):
         @pl.when((time >= 1) & (time - 1 < STEPS))
@@ -394,7 +1209,12 @@
 
             @pl.when((half == 0) & ((unit < 5) | (unit == 8) | (unit == 9) | (unit == 12)))
             def _():
-                pltpu.make_async_copy(a_hbm.at[slot_a], a_vmem.at[slot_a], a_sem.at[slot_a]).wait()
+                pltpu.make_async_copy(a_hbm.at[slot_a], a_raw, a_sem).wait()
+                a_vmem[...] = a_raw[...].T
+
+                @pl.when(slot_a + 1 < FACTOR_A)
+                def _():
+                    pltpu.make_async_copy(a_hbm.at[slot_a + 1], a_raw, a_sem).start()
 
             @pl.when((half == 0) & ((unit == 0) | (unit >= 4)))
             def _():
@@ -405,13 +1225,13 @@
                 rows = pl.ds(
                     pl.multiple_of(which * HALF + (1 - core) * QUARTER + half * ROWS, ROWS), ROWS
                 )
-                core_out[step % 2, which] = low(product(a_vmem[slot_a, rows], right))
+                core_out[step % 2, which] = low(product(a_vmem[rows], right))
             core_copy(step).start()
             for which in range(2):
                 rows = pl.ds(
                     pl.multiple_of(which * HALF + core * QUARTER + half * ROWS, ROWS), ROWS
                 )
-                part[step, which] = low(product(a_vmem[slot_a, rows], right))
+                part[step, which] = low(product(a_vmem[rows], right))
 
         @pl.when((time >= 2) & (time - 2 < STEPS))
         def _():
@@ -541,57 +1361,38 @@
         out_copy(step, 1 - core).wait()
 
 
-def reduce_kernel(factors, vectors):
-    (normed, triple_grad), (attended, mix_low), (normed_two, pre_low), (active, down_low), last = (
-        factors
-    )
-    pooled, embed_grad = last
-    rows = normed.shape[0]
-    active_t = active.T.reshape(2, 4, HALF, rows).transpose(1, 0, 2, 3).reshape(4, WIDTH, rows)
-    pooled_t = jnp.pad(pooled.T, ((0, 0), (0, rows - pooled.shape[0])))
-    left = jnp.concatenate(
-        [active_t, normed_two.T[None], attended.T[None], normed.T[None], pooled_t[None]], axis=0
-    )
-    right = jnp.concatenate(
-        [
-            down_low[None],
-            pre_low.reshape(rows, 4, WIDTH).transpose(1, 0, 2),
-            mix_low[None],
-            triple_grad.reshape(rows, 3, WIDTH).transpose(1, 0, 2),
-            jnp.pad(embed_grad, ((0, rows - embed_grad.shape[0]), (0, 0)))[None],
-        ],
-        axis=0,
-    )
-    packed = jnp.concatenate([vector.reshape(-1, WIDTH) for vector in vectors], axis=0)
-    packed = jnp.pad(packed, ((0, VECTOR_ROWS - packed.shape[0]), (0, 0)))
+def reduce_kernel(left, right, packed):
+    rows = left.shape[1]
     any_spec = pl.BlockSpec(memory_space=pl.ANY)
     vmem_spec = pl.BlockSpec(memory_space=pltpu.VMEM)
     dma = pltpu.SemaphoreType.DMA
-    grads, packed = pl.pallas_call(
+    low_type = jnp.bfloat16
+    return pl.pallas_call(
         reduce_body,
         out_shape=(
-            jax.ShapeDtypeStruct((UNITS, HALF, WIDTH), jnp.bfloat16),
+            jax.ShapeDtypeStruct((UNITS, HALF, WIDTH), low_type),
             jax.ShapeDtypeStruct((VECTOR_ROWS, WIDTH), jnp.float32),
         ),
         in_specs=[any_spec, any_spec, vmem_spec],
         out_specs=(any_spec, vmem_spec),
         scratch_shapes=[
-            pltpu.VMEM((FACTOR_A, WIDTH, rows), jnp.bfloat16),
-            pltpu.VMEM((FACTOR_B, rows, WIDTH), jnp.bfloat16),
-            pltpu.VMEM((2, 2, ROWS, WIDTH), jnp.bfloat16),
-            pltpu.VMEM((STEPS, 2, ROWS, WIDTH), jnp.bfloat16),
-            pltpu.VMEM((STEPS, 2, ROWS, WIDTH), jnp.bfloat16),
-            pltpu.VMEM((STEPS, ROWS, WIDTH), jnp.bfloat16),
-            pltpu.VMEM((STEPS, PART, WIDTH), jnp.bfloat16),
-            pltpu.VMEM((STEPS, PART, WIDTH), jnp.bfloat16),
-            pltpu.VMEM((STEPS, PART, WIDTH), jnp.bfloat16),
-            pltpu.VMEM((STEPS, 2, ROWS, WIDTH), jnp.bfloat16),
+            pltpu.VMEM((rows, WIDTH), low_type),
+            pltpu.VMEM((WIDTH, rows), low_type),
+            pltpu.VMEM((FACTOR_B, rows, WIDTH), low_type),
+            pltpu.VMEM((2, 2, ROWS, WIDTH), low_type),
+            pltpu.VMEM((STEPS, 2, ROWS, WIDTH), low_type),
+            pltpu.VMEM((STEPS, 2, ROWS, WIDTH), low_type),
+            pltpu.VMEM((STEPS, ROWS, WIDTH), low_type),
+            pltpu.VMEM((STEPS, PART, WIDTH), low_type),
+            pltpu.VMEM((STEPS, PART, WIDTH), low_type),
+            pltpu.VMEM((STEPS, PART, WIDTH), low_type),
+            pltpu.VMEM((STEPS, 2, ROWS, WIDTH), low_type),
             pltpu.VMEM((VECTOR_ROWS, WIDTH), jnp.float32),
             pltpu.VMEM((VECTOR_ROWS, WIDTH), jnp.float32),
             pltpu.VMEM((VECTOR_ROWS, WIDTH), jnp.float32),
             pltpu.VMEM((3, VECTOR_ROWS, WIDTH), jnp.float32),
             pltpu.VMEM((3, VECTOR_ROWS, WIDTH), jnp.float32),
-            dma((FACTOR_A,)),
+            dma(()),
             dma((FACTOR_B,)),
             dma((2, STEPS)),
             dma((2, STEPS)),
@@ -605,35 +1406,118 @@
             dma((2, 6)),
         ],
         compiler_params=pltpu.CompilerParams(
-            collective_id=0, has_side_effects=True, vmem_limit_bytes=62 * 1024 * 1024
+            collective_id=0, has_side_effects=True, vmem_limit_bytes=60 * 1024 * 1024
         ),
     )(left, right, packed)
+
+
+def finish_body(grad_hbm, packed_ref, *refs):
+    (
+        gain,
+        offset,
+        joint,
+        mixer,
+        mix_bias,
+        feed_gain,
+        feed_offset,
+        up,
+        up_bias,
+        down,
+        down_bias,
+        end_gain,
+        end_offset,
+        project,
+        scale_out,
+        loss_out,
+        low_values,
+        wide_values,
+        load_sem,
+        store_sem,
+    ) = refs
     shard = lax.axis_index("fsdp")
-    wide = grads.astype(jnp.float32)
-
-    def matrix(first, count):
-        return wide[first : first + count].transpose(1, 0, 2).reshape(HALF, count * WIDTH)
-
-    def vector(first, count):
-        full = packed[first : first + count].reshape(2, count * HALF)
-        return lax.dynamic_index_in_dim(full, shard, 0, keepdims=False)
-
-    return (
-        vector(0, 1),
-        vector(1, 1),
-        matrix(9, 3),
-        matrix(8, 1),
-        vector(2, 1),
-        vector(3, 1),
-        vector(4, 1),
-        matrix(4, 4),
-        vector(5, 4),
-        wide[0:4].reshape(4 * HALF, WIDTH),
-        vector(9, 1),
-        vector(10, 1),
-        vector(11, 1),
-        matrix(12, 1),
-    )
+    loads = [
+        pltpu.make_async_copy(grad_hbm.at[unit], low_values.at[unit], load_sem.at[unit])
+        for unit in range(UNITS)
+    ]
+    for load in loads:
+        load.start()
+    for row, target in (
+        (0, gain),
+        (1, offset),
+        (2, mix_bias),
+        (3, feed_gain),
+        (4, feed_offset),
+        (9, down_bias),
+        (10, end_gain),
+        (11, end_offset),
+    ):
+        cols = pl.ds(pl.multiple_of(shard * HALF, HALF), HALF)
+        target[...] = packed_ref[pl.ds(row, 1), cols].reshape(HALF)
+    for part in range(2):
+        up_bias[pl.ds(part * WIDTH, WIDTH)] = packed_ref[
+            pl.ds(5 + 2 * shard + part, 1), :
+        ].reshape(WIDTH)
+    loss_out[...] = packed_ref[12:13, 0:1]
+    scale_out[...] = packed_ref[12:13, 1:2]
+    places = (
+        [(down, pl.ds(unit * HALF, HALF), pl.ds(0, WIDTH)) for unit in range(4)]
+        + [(up, pl.ds(0, HALF), pl.ds(unit * WIDTH, WIDTH)) for unit in range(4)]
+        + [(mixer, pl.ds(0, HALF), pl.ds(0, WIDTH))]
+        + [(joint, pl.ds(0, HALF), pl.ds(unit * WIDTH, WIDTH)) for unit in range(3)]
+        + [(project, pl.ds(0, HALF), pl.ds(0, WIDTH))]
+    )
+    stores = []
+    for unit, (target, rows, cols) in enumerate(places):
+        loads[unit].wait()
+        wide_values[unit] = wide(low_values[unit])
+        copy = pltpu.make_async_copy(wide_values.at[unit], target.at[rows, cols], store_sem.at[unit])
+        copy.start()
+        stores.append(copy)
+    for copy in stores:
+        copy.wait()
+
+
+def finish_kernel(grads, packed):
+    single = jnp.float32
+    any_spec = pl.BlockSpec(memory_space=pl.ANY)
+    vmem_spec = pl.BlockSpec(memory_space=pltpu.VMEM)
+    vector = (jax.ShapeDtypeStruct((HALF,), single), vmem_spec)
+    scalar = (jax.ShapeDtypeStruct((1, 1), single), vmem_spec)
+
+    def matrix(rows, cols):
+        return (jax.ShapeDtypeStruct((rows, cols), single), any_spec)
+
+    outs = (
+        vector,
+        vector,
+        matrix(HALF, 3 * WIDTH),
+        matrix(HALF, WIDTH),
+        vector,
+        vector,
+        vector,
+        matrix(HALF, 4 * WIDTH),
+        (jax.ShapeDtypeStruct((4 * HALF,), single), vmem_spec),
+        matrix(4 * HALF, WIDTH),
+        vector,
+        vector,
+        vector,
+        matrix(HALF, WIDTH),
+        scalar,
+        scalar,
+    )
+    return pl.pallas_call(
+        finish_body,
+        out_shape=tuple(shape for shape, spec in outs),
+        in_specs=[any_spec, vmem_spec],
+        out_specs=tuple(spec for shape, spec in outs),
+        scratch_shapes=[
+            pltpu.VMEM((UNITS, HALF, WIDTH), jnp.bfloat16),
+            pltpu.VMEM((UNITS, HALF, WIDTH), single),
+            pltpu.SemaphoreType.DMA((UNITS,)),
+            pltpu.SemaphoreType.DMA((UNITS,)),
+        ],
+        compiler_params=pltpu.CompilerParams(vmem_limit_bytes=48 * 1024 * 1024),
+    )(grads, packed)
 
 
 def reduce_plain(factors, vectors):
@@ -662,40 +1546,41 @@
     return lax.psum(shards, "dp")
 
 
-def on_device(
-    text_tokens,
-    image_tokens,
-    pair_counts,
-    log_scale,
-    text_gain,
-    text_offset,
-    text_joint,
-    text_mixer,
-    text_mixbias,
-    text_feedgain,
-    text_feedoffset,
-    text_upward,
-    text_upbias,
-    text_downward,
-    text_downbias,
-    text_endgain,
-    text_endoffset,
-    text_project,
-    image_gain,
-    image_offset,
-    image_joint,
-    image_mixer,
-    image_mixbias,
-    image_feedgain,
-    image_feedoffset,
-    image_upward,
-    image_upbias,
-    image_downward,
-    image_downbias,
-    image_endgain,
-    image_endoffset,
-    image_project,
-):
+def on_device_plain(*arrays):
+    (
+        text_tokens,
+        image_tokens,
+        pair_counts,
+        log_scale,
+        text_gain,
+        text_offset,
+        text_joint,
+        text_mixer,
+        text_mixbias,
+        text_feedgain,
+        text_feedoffset,
+        text_upward,
+        text_upbias,
+        text_downward,
+        text_downbias,
+        text_endgain,
+        text_endoffset,
+        text_project,
+        image_gain,
+        image_offset,
+        image_joint,
+        image_mixer,
+        image_mixbias,
+        image_feedgain,
+        image_feedoffset,
+        image_upward,
+        image_upbias,
+        image_downward,
+        image_downbias,
+        image_endgain,
+        image_endoffset,
+        image_project,
+    ) = arrays
     image_weights = (
         image_gain,
         image_offset,
@@ -773,16 +1658,41 @@
     factors, vectors, token_grad = backward_block(
         kept_values, text_weights, unit_grad, TEXT_LEN
     )
-    if (lax.axis_size("dp"), lax.axis_size("fsdp")) == (16, 2):
-        final_grads = reduce_kernel(factors, vectors)
-    else:
-        final_grads = reduce_plain(factors, vectors)
+    final_grads = reduce_plain(factors, vectors)
     return (
         *final_grads,
         jnp.reshape(scale_total, (1,)),
         token_grad,
         jnp.reshape(loss_total, (1,)),
     )
+
+
+def on_device(*arrays):
+    if (lax.axis_size("dp"), lax.axis_size("fsdp")) != (16, 2):
+        return on_device_plain(*arrays)
+    text_tokens, image_tokens, pair_counts, log_scale = arrays[:4]
+    text_weights, image_weights = arrays[4:18], arrays[18:32]
+    matrix_places = (2, 3, 7, 9, 13)
+    vector_places = (0, 1, 4, 5, 6, 10, 11, 12)
+    shard_vector = jnp.concatenate(
+        [jnp.stack([text_weights[place] for place in vector_places])]
+        + [text_weights[8].reshape(4, HALF), jnp.zeros((4, HALF), jnp.bfloat16)],
+        axis=0,
+    ).reshape(VECTOR_ROWS, 1, HALF)
+    shards = tuple(text_weights[place] for place in matrix_places)
+    image_low, vectors, matrices = image_kernel(image_tokens, image_weights, shard_vector, shards)
+    slots = jnp.arange(SLOT_ROWS)[None, :]
+    counts = pair_counts.reshape(4, 2, 2, 2).transpose(2, 1, 3, 0).reshape(-1)
+    live = ((slots < SLOTS) & (slots < counts[:, None])).astype(jnp.float32).reshape(1, -1)
+    device = lax.axis_index("dp") * lax.axis_size("fsdp") + lax.axis_index("fsdp")
+    own_count = lax.dynamic_index_in_dim(pair_counts, device, 0, keepdims=False)
+    own_live = (jnp.arange(SLOTS) < own_count).astype(jnp.float32)[:, None]
+    left, right, packed, token_grad = text_kernel(
+        text_tokens, vectors, image_low, live, own_live, log_scale, matrices
+    )
+    grads, packed = reduce_kernel(left, right, packed)
+    *final_grads, scale_total, loss_total = finish_kernel(grads, packed)
+    return (*final_grads, scale_total.reshape(1), token_grad, loss_total.reshape(1))
 
 
 def solution(mesh):

time: 863 us -> 482 us (0.56)
  Pallas kernels: 120 us -> 449 us
  local copies, waits for them, and re-layouts: 214 us -> 20.7 us
  waiting for transfers between devices: 164 us -> 0 us
  matrix products: 133 us -> 0 us
  blocking collectives: 118 us -> 0 us
  other arithmetic: 83.2 us -> 1.33 us
  between operations: 20.4 us -> 1.82 us
    pallas_call x0 -> x3, Pallas kernels: none -> 328 us  [the longest x1 239 us: image_kernel(): pl.pallas_call(image_body, out_shape=(jax.ShapeDtypeStruct((blocks, IMAGE...]
    all_gather x6 -> x0, waiting for transfers between devices: 161 us -> none  [the longest x5 153 us: on_device(): lax.all_gather(shard, 'fsdp', axis=0, tiled=True)]
    dot_general x24 -> x0, matrix products: 133 us -> none  [the longest x10 76.3 us: product(): return jnp.dot(left_side, right_side, preferred_element_type=jnp.float32)]
    psum x2 -> x0, blocking collectives: 77.8 us -> none  [the longest x1 39.4 us: on_device(): column_sum = lax.psum(column_sum, ('dp', 'fsdp'))]
    reshape x24 -> x5, local copies, waits for them, and re-layouts: 60.6 us -> 4.28 us  [the longest x1 1.3 us: image_kernel(): up_bias.reshape(1, feed)]
    all_gather x9 -> x0, blocking collectives: 40.2 us -> none  [on_device(): lax.all_gather(shard, 'fsdp', axis=0, tiled=True)]
    unnamed x171 -> x5, local copies, waits for them, and re-layouts: 37.7 us -> 2 us
    convert_element_type x15 -> x1, local copies, waits for them, and re-layouts: 32 us -> 0.69 us  [on_device(): ((slots < SLOTS) & (slots < counts[:, None])).astype(jnp.float32)]
  transfers between devices with their start and end apart: 6 -> 0, of which waited for: 5 -> 0; matrix products, arithmetic and copies ran while one was open for 9% -> 0% of each run, Pallas kernels for 0% -> 0%
where the time goes in v2:
time: 482 us; the launch traced here: 473 us
  Pallas kernels  449 us (93%)
  local copies, waits for them, and re-layouts  20.7 us (4%)
    pallas_call x1, Pallas kernels, image_kernel(): pl.pallas_call(image_body, out_shape=(jax.ShapeDtypeStruct((blocks, IMAGE...  239 us
    pallas_call x1, Pallas kernels, reduce_kernel(): pl.pallas_call(reduce_body, out_shape=(jax.ShapeDtypeStruct((UNITS, HALF,...  121 us
    pallas_call x1, Pallas kernels, text_kernel(): pl.pallas_call(text_body, out_shape=(jax.ShapeDtypeStruct((FACTOR_A, rows...  79.9 us

profile of v2, /device:TPU:0, one launch (start us, length us, event | category | flops | bytes accessed | tf_op | source)
XLA Modules:
  0.0 473.0 jit_solution(17524509071109913874)
XLA Ops:
  1.3 1.2 dynamic_slice.4
  2.6 0.7 stack.60
  3.2 0.7 stack.61
  3.9 0.7 stack.62
  4.6 0.7 stack.63
  5.3 0.7 stack.64
  6.0 0.7 stack.65
  6.6 0.7 stack.66
  7.3 0.7 stack.67
  8.0 0.7 reshape.120
  8.7 0.7 stack.51
  9.4 0.7 stack.52
  10.1 0.7 stack.53
  10.8 0.7 stack.54
  11.5 0.7 stack.55
  12.1 0.7 stack.56
  12.8 0.7 stack.57
  13.5 0.7 stack.58
  14.2 0.6 stack.59.vector_ref
  14.8 0.1 concatenate.3
  14.9 0.7 reshape.123
  15.7 0.1 copy.51
  15.8 0.1 lt.54
  15.9 0.6 copy.50.shard_vector
  16.5 1.3 reshape.119.bias_ref
  17.8 0.1 fusion.2
  17.9 0.7 reshape.127.live_ref
  18.6 1.3 fusion.own_live_ref
  19.8 239.2 %shard_map.431 = (bf16[3,12,768]{2,1,0:T(8,128)(2,1)}, bf16[2,16,1,384]{3,2,1,0:T(2,128)(2,1)}, bf16[768,2304]{1,0:T(8,128)(2,1)}, bf16[768,768]{1,0:T(8,128)(2,...) custom-call(bf16[3,600,768]{2,1,0:T(8,128)(2,1)} %bitcast.8, ...), custom_call_target="tpu_custom_call" | custom-call | tf_op jit(solution)/shard_map/pallas_call | solution.py:1022
  259.1 0.9 reshape.122
  260.0 0.6 pad.4.image_ref
  260.6 79.9 %shard_map.432 = (bf16[8,576,768]{2,1,0:T(8,128)(2,1)}, bf16[10,576,768]{2,1,0:T(8,128)(2,1)}, f32[16,768]{1,0:T(8,128)}, f32[576,768]{1,0:T(8,128)}) custom-call(bf16[576,768]{1,0:T(8,128)(2,1)} %token_ref.1, bf16[2,16,1,384]{3,2,1,0:T(2,128)(2,1)} %get-tuple-element.46.vector_ref, bf16[40,768]{1,0:T(8,128)(2,1)} %pad.4.image_ref, ...), custom_call_target="tpu_custom_call" | custom-call | tf_op jit(solution)/shard_map/pallas_call | solution.py:679
  340.5 121.3 %shard_map.433 = (bf16[13,384,768]{2,1,0:T(8,128)(2,1)}, f32[16,768]{1,0:T(8,128)}) custom-call(bf16[8,576,768]{2,1,0:T(8,128)(2,1)} %get-tuple-element.53.a_hbm, bf16[10,576,768]{2,1,0:T(8,128)(2,1)} %get-tuple-element.54.b_hbm, f32[16,768]{1,0:T(8,128)} %get-tuple-element.55.vector_ref), custom_call_target="tpu_custom_call" | custom-call | tf_op jit(solution)/shard_map/pallas_call | solution.py:1370
  461.8 0.0 copy-start
  461.8 0.8 copy-done
  462.6 0.0 copy-start.1
  462.6 8.7 %shard_map.434 = (f32[384]{0:T(512)}, f32[384]{0:T(512)}, f32[384,2304]{1,0:T(8,128)}, f32[384,768]{1,0:T(8,128)}, f32[384]{0:T(512)}, /*index=5*/f32[384]{0:T(5...) custom-call(bf16[13,384,768]{2,1,0:T(8,128)(2,1)} %get-tuple-element, ...), custom_call_target="tpu_custom_call" | custom-call | tf_op jit(solution)/shard_map/pallas_call | solution.py:1508
  471.3 0.0 copy-done.1
  471.3 1.2 copy.54
  (2 shorter events, 0.0 us)
Async XLA Ops:
  461.8 0.8 copy-start
  462.6 8.7 %copy-start.1 = (f32[576,768]{1,0:T(8,128)S(1)}, f32[576,768]{1,0:T(8,128)}, u32[]{:S(2)}) copy-start(f32[576,768]{1,0:T(8,128)} %get-tuple-element.107) | copy-start | bytes 5308420
